TPU v7x, 32 devices: a whole 2x2x4 slice. The times are simulated.
32 devices in a mesh: ctx: 4 (over y, x), fsdp: 8 (over z, core).
Axes of the slice: x: 2, y: 2, z: 4, core: 2. Of those that a mesh axis runs over, the one named last changes fastest.
Arguments:
- tokens: bfloat16 [8, 1024, 1024], P('fsdp', 'ctx'), may hold values from -6 to 6
- positions: int32 [8, 1024], P('fsdp', 'ctx'), may hold values from 0 to 511, as said below
- block_pairs: int32 [4], replicated, may hold values from 0 to 3, as said below
- input_gain: bfloat16 [1024], P('fsdp'), may hold values from 0.5 to 1.5
- query_gain: bfloat16 [64], P('fsdp'), may hold values from 0.5 to 1.5
- key_gain: bfloat16 [64], P('fsdp'), may hold values from 0.5 to 1.5
- query_weight: bfloat16 [1024, 1024], P('fsdp'), may hold values from -0.1875 to 0.1875
- key_weight: bfloat16 [1024, 512], P('fsdp'), may hold values from -0.1875 to 0.1875
- value_weight: bfloat16 [1024, 512], P('fsdp'), may hold values from -0.1875 to 0.1875
- out_weight: bfloat16 [1024, 1024], P('fsdp'), may hold values from -2 to 2
- middle_gain: bfloat16 [1024], P('fsdp'), may hold values from 0.5 to 1.5
- gate_weight: bfloat16 [1024, 4608], P('fsdp'), may hold values from -0.1875 to 0.1875
- up_weight: bfloat16 [1024, 4608], P('fsdp'), may hold values from -0.1875 to 0.1875
- down_weight: bfloat16 [4608, 1024], P('fsdp'), may hold values from -0.09375 to 0.09375
- cotangent: bfloat16 [8, 1024, 1024], P('fsdp', 'ctx'), may hold values from -6 to 6
Outputs:
- layer_out: bfloat16 [8, 1024, 1024], P('fsdp', 'ctx')
- grad_tokens: bfloat16 [8, 1024, 1024], P('fsdp', 'ctx')
- grad_input_gain: float32 [1024], P('fsdp')
- grad_query_gain: float32 [64], P('fsdp')
- grad_key_gain: float32 [64], P('fsdp')
- grad_query_weight: float32 [1024, 1024], P('fsdp')
- grad_key_weight: float32 [1024, 512], P('fsdp')
- grad_value_weight: float32 [1024, 512], P('fsdp')
- grad_out_weight: float32 [1024, 1024], P('fsdp')
- grad_middle_gain: float32 [1024], P('fsdp')
- grad_gate_weight: float32 [1024, 4608], P('fsdp')
- grad_up_weight: float32 [1024, 4608], P('fsdp')
- grad_down_weight: float32 [4608, 1024], P('fsdp')
Inputs may be any that keep to these rules, and one draw needn't show every extreme that they name: A permutation; in every sequence, index c of ctx holds the blocks of 128 tokens numbered block_pairs[c] and 7 - block_pairs[c] in true order, in that order. `positions`: each row's place within its document, documents following one another in true order; the first document of a sequence covers its first 512 tokens in true order, and a document starts at true place 1024 // 2.
All inputs are finite; a program needn't handle non-finite values.
Results may differ from a plain program's by a relative error of at most 0.025.
Values may be sent and summed in bfloat16 or wider, within the bound.
No kernel may reach another device: no remote copies, remote signals or barrier semaphores. Data moves between devices by JAX's collectives and lax.ppermute only.
A program may use at most 192 MiB of HBM per device.

v0:
```python
import jax
import jax.numpy as jnp
from jax import lax
from jax.sharding import PartitionSpec as P

H = 16
HD = 64
KV = 8


epsilon = 1e-05
theta_base = 1000000.0
score_scale = 0.125
masked_value = -1e30


def dot_plain(left, right):
    return jnp.dot(left, right, preferred_element_type=jnp.float32)


def times_transposed(left, right):
    return lax.dot_general(
        left, right, (((1,), (1,)), ((), ())), preferred_element_type=jnp.float32
    )


def transposed_times(left, right):
    return lax.dot_general(
        left, right, (((0,), (0,)), ((), ())), preferred_element_type=jnp.float32
    )


def norm_forward(values, scale_vec):
    inverse = lax.rsqrt(jnp.mean(values * values, axis=-1, keepdims=True) + epsilon)
    normal = values * inverse
    return (normal * scale_vec, normal, inverse)


def norm_backward(upstream, normal, inverse, scale_vec):
    scaled = upstream * scale_vec
    inner = jnp.mean(scaled * normal, axis=-1, keepdims=True)
    return (inverse * (scaled - normal * inner), upstream * normal)


def rotate(values, places, direction):
    half_dim = HD // 2
    freqs = theta_base ** (-(jnp.arange(half_dim, dtype=jnp.float32) * 2.0) / HD)
    angles = places.astype(jnp.float32)[:, None] * freqs[None, :]
    cosine = jnp.cos(angles)[:, None, :]
    sine = direction * jnp.sin(angles)[:, None, :]
    first_half = values[..., :half_dim]
    second_half = values[..., half_dim:]
    return jnp.concatenate(
        [first_half * cosine - second_half * sine, second_half * cosine + first_half * sine],
        axis=-1,
    )


def true_places(block_pairs, rank_count, rows_each):
    half_rows = rows_each // 2
    row_ids = jnp.arange(rank_count * rows_each, dtype=jnp.int32)
    owner = row_ids // rows_each
    within = row_ids % rows_each
    ranks_row = jnp.arange(rank_count, dtype=jnp.int32)
    picked = jnp.sum(
        jnp.where(owner[:, None] == ranks_row[None, :], block_pairs[None, :], 0), axis=1
    )
    blocks_of = jnp.where(within < half_rows, picked, 2 * rank_count - 1 - picked)
    return blocks_of * half_rows + within % half_rows


def swiglu_grads(act_grad, gate, up_values, sigma, swish):
    gate_grad = (act_grad * up_values * sigma * (1.0 + gate * (1.0 - sigma))).astype(jnp.bfloat16)
    up_grad = (act_grad * swish).astype(jnp.bfloat16)
    return (gate_grad, up_grad)


def shards(
    tokens,
    positions,
    block_pairs,
    input_gain,
    query_gain,
    key_gain,
    query_weight,
    key_weight,
    value_weight,
    out_weight,
    middle_gain,
    gate_weight,
    up_weight,
    down_weight,
    cotangent,
):
    rank_count = lax.axis_size("ctx")
    my_rank = lax.axis_index("ctx")
    hidden = tokens[0].astype(jnp.float32)
    places = positions[0]
    rows_here = hidden.shape[0]
    groups = H // KV
    order_all = true_places(block_pairs, rank_count, rows_here)
    order_own = lax.dynamic_slice_in_dim(order_all, my_rank * rows_here, rows_here)
    allowed = order_own[:, None] >= order_all[None, :]
    attn_set = (
        lax.all_gather(input_gain, "fsdp", axis=0, tiled=True),
        lax.all_gather(query_gain, "fsdp", axis=0, tiled=True),
        lax.all_gather(key_gain, "fsdp", axis=0, tiled=True),
        lax.all_gather(middle_gain, "fsdp", axis=0, tiled=True),
        lax.all_gather(query_weight, "fsdp", axis=0, tiled=True),
        lax.all_gather(key_weight, "fsdp", axis=0, tiled=True),
        lax.all_gather(value_weight, "fsdp", axis=0, tiled=True),
        lax.all_gather(out_weight, "fsdp", axis=0, tiled=True),
    )
    gain_one = attn_set[0].astype(jnp.float32)
    gain_query = attn_set[1].astype(jnp.float32)
    gain_key = attn_set[2].astype(jnp.float32)
    gain_two = attn_set[3].astype(jnp.float32)
    normed_full, normal_one, inverse_one = norm_forward(hidden, gain_one)
    normed = normed_full.astype(jnp.bfloat16)
    query_proj = dot_plain(normed, attn_set[4]).reshape(rows_here, H, HD)
    key_proj = dot_plain(normed, attn_set[5]).reshape(rows_here, KV, HD)
    value_rows = dot_plain(normed, attn_set[6]).astype(jnp.bfloat16)
    query_normed, query_unit, query_inverse = norm_forward(query_proj, gain_query)
    key_normed, key_unit, key_inverse = norm_forward(key_proj, gain_key)
    query_rot = (
        rotate(query_normed, places, 1.0).astype(jnp.bfloat16).reshape(rows_here, KV, groups, HD)
    )
    key_rot = rotate(key_normed, places, 1.0).astype(jnp.bfloat16).reshape(rows_here, KV * HD)
    keys_flat, values_flat = (
        lax.all_gather(key_rot, "ctx", axis=0, tiled=True),
        lax.all_gather(value_rows, "ctx", axis=0, tiled=True),
    )
    keys_all = keys_flat.reshape(-1, KV, HD)
    values_all = values_flat.reshape(-1, KV, HD)

    def attention_scores():
        raw = (
            jnp.einsum("qgrd,kgd->grqk", query_rot, keys_all, preferred_element_type=jnp.float32)
            * score_scale
        )
        return jnp.where(allowed[None, None], raw, masked_value)

    scores = attention_scores()
    row_top = jnp.max(scores, axis=-1, keepdims=True)
    expo = jnp.exp(scores - row_top)
    denominator = jnp.sum(expo, axis=-1, keepdims=True)
    log_total = row_top + jnp.log(denominator)
    probs_low = (expo / denominator).astype(jnp.bfloat16)
    mixed = (
        jnp.einsum("grqk,kgd->qgrd", probs_low, values_all, preferred_element_type=jnp.float32)
        .reshape(rows_here, H * HD)
        .astype(jnp.bfloat16)
    )
    middle = hidden + dot_plain(mixed, attn_set[7])
    normed_two_full, normal_two, inverse_two = norm_forward(middle, gain_two)
    normed_two = normed_two_full.astype(jnp.bfloat16)
    upstream = cotangent[0]
    upstream_full = upstream.astype(jnp.float32)
    ffn_set = (
        lax.all_gather(gate_weight, "fsdp", axis=0, tiled=True),
        lax.all_gather(up_weight, "fsdp", axis=0, tiled=True),
        lax.all_gather(down_weight, "fsdp", axis=0, tiled=True),
    )
    gate = dot_plain(normed_two, ffn_set[0])
    up_values = dot_plain(normed_two, ffn_set[1])
    sigma = jax.nn.sigmoid(gate)
    swish = gate * sigma
    act_low = (swish * up_values).astype(jnp.bfloat16)
    result = (middle + dot_plain(act_low, ffn_set[2])).astype(jnp.bfloat16)
    act_grad = times_transposed(upstream, ffn_set[2])
    gate_grad, up_grad = swiglu_grads(act_grad, gate, up_values, sigma, swish)
    local_down = transposed_times(act_low, upstream)
    local_gate = transposed_times(normed_two, gate_grad)
    local_up = transposed_times(normed_two, up_grad)
    normed_two_grad = times_transposed(gate_grad, ffn_set[0]) + times_transposed(
        up_grad, ffn_set[1]
    )
    grad_gate, grad_up, grad_down = (
        lax.psum_scatter(
            local_gate.astype(jnp.bfloat16), "fsdp", scatter_dimension=0, tiled=True
        ).astype(jnp.float32),
        lax.psum_scatter(
            local_up.astype(jnp.bfloat16), "fsdp", scatter_dimension=0, tiled=True
        ).astype(jnp.float32),
        lax.psum_scatter(
            local_down.astype(jnp.bfloat16), "fsdp", scatter_dimension=0, tiled=True
        ).astype(jnp.float32),
    )
    middle_part, gain_two_terms = norm_backward(normed_two_grad, normal_two, inverse_two, gain_two)
    middle_grad = upstream_full + middle_part
    attn_back = (
        lax.all_gather(input_gain, "fsdp", axis=0, tiled=True),
        lax.all_gather(query_gain, "fsdp", axis=0, tiled=True),
        lax.all_gather(key_gain, "fsdp", axis=0, tiled=True),
        lax.all_gather(middle_gain, "fsdp", axis=0, tiled=True),
        lax.all_gather(query_weight, "fsdp", axis=0, tiled=True),
        lax.all_gather(key_weight, "fsdp", axis=0, tiled=True),
        lax.all_gather(value_weight, "fsdp", axis=0, tiled=True),
        lax.all_gather(out_weight, "fsdp", axis=0, tiled=True),
    )
    middle_low = middle_grad.astype(jnp.bfloat16)
    grad_out = transposed_times(mixed, middle_low)
    mixed_grad = (
        times_transposed(middle_low, attn_back[7])
        .astype(jnp.bfloat16)
        .reshape(rows_here, KV, groups, HD)
    )
    probs_again = jnp.exp(attention_scores() - log_total)
    prob_grad = jnp.einsum(
        "qgrd,kgd->grqk", mixed_grad, values_all, preferred_element_type=jnp.float32
    )
    row_inner = jnp.sum(probs_again * prob_grad, axis=-1, keepdims=True)
    score_grad = (probs_again * (prob_grad - row_inner)).astype(jnp.bfloat16)
    probs_low_again = probs_again.astype(jnp.bfloat16)
    query_grad_rot = (
        jnp.einsum("grqk,kgd->qgrd", score_grad, keys_all, preferred_element_type=jnp.float32)
        * score_scale
    )
    key_part = (
        jnp.einsum("grqk,qgrd->kgd", score_grad, query_rot, preferred_element_type=jnp.float32)
        * score_scale
    )
    value_part = jnp.einsum(
        "grqk,qgrd->kgd", probs_low_again, mixed_grad, preferred_element_type=jnp.float32
    )
    key_grad_rot, value_grad = (
        lax.psum_scatter(
            key_part.reshape(-1, KV * HD).astype(jnp.bfloat16),
            "ctx",
            scatter_dimension=0,
            tiled=True,
        ).astype(jnp.float32),
        lax.psum_scatter(
            value_part.reshape(-1, KV * HD).astype(jnp.bfloat16),
            "ctx",
            scatter_dimension=0,
            tiled=True,
        ).astype(jnp.float32),
    )
    query_normed_grad = rotate(query_grad_rot.reshape(rows_here, H, HD), places, -1.0)
    key_normed_grad = rotate(key_grad_rot.reshape(rows_here, KV, HD), places, -1.0)
    query_proj_grad, query_gain_terms = norm_backward(
        query_normed_grad, query_unit, query_inverse, attn_back[1].astype(jnp.float32)
    )
    key_proj_grad, key_gain_terms = norm_backward(
        key_normed_grad, key_unit, key_inverse, attn_back[2].astype(jnp.float32)
    )
    query_grad_low = query_proj_grad.reshape(rows_here, H * HD).astype(jnp.bfloat16)
    key_grad_low = key_proj_grad.reshape(rows_here, KV * HD).astype(jnp.bfloat16)
    value_grad_low = value_grad.astype(jnp.bfloat16)
    grad_query = transposed_times(normed, query_grad_low)
    grad_key = transposed_times(normed, key_grad_low)
    grad_value = transposed_times(normed, value_grad_low)
    normed_grad = (
        times_transposed(query_grad_low, attn_back[4])
        + times_transposed(key_grad_low, attn_back[5])
        + times_transposed(value_grad_low, attn_back[6])
    )
    hidden_part, gain_one_terms = norm_backward(
        normed_grad, normal_one, inverse_one, attn_back[0].astype(jnp.float32)
    )
    input_grad = (middle_grad + hidden_part).astype(jnp.bfloat16)
    attn_shares = (
        lax.psum_scatter(
            jnp.sum(gain_one_terms, axis=0).astype(jnp.bfloat16),
            "fsdp",
            scatter_dimension=0,
            tiled=True,
        ).astype(jnp.float32),
        lax.psum_scatter(
            jnp.sum(query_gain_terms, axis=(0, 1)).astype(jnp.bfloat16),
            "fsdp",
            scatter_dimension=0,
            tiled=True,
        ).astype(jnp.float32),
        lax.psum_scatter(
            jnp.sum(key_gain_terms, axis=(0, 1)).astype(jnp.bfloat16),
            "fsdp",
            scatter_dimension=0,
            tiled=True,
        ).astype(jnp.float32),
        lax.psum_scatter(
            jnp.sum(gain_two_terms, axis=0).astype(jnp.bfloat16),
            "fsdp",
            scatter_dimension=0,
            tiled=True,
        ).astype(jnp.float32),
        lax.psum_scatter(
            grad_query.astype(jnp.bfloat16), "fsdp", scatter_dimension=0, tiled=True
        ).astype(jnp.float32),
        lax.psum_scatter(
            grad_key.astype(jnp.bfloat16), "fsdp", scatter_dimension=0, tiled=True
        ).astype(jnp.float32),
        lax.psum_scatter(
            grad_value.astype(jnp.bfloat16), "fsdp", scatter_dimension=0, tiled=True
        ).astype(jnp.float32),
        lax.psum_scatter(
            grad_out.astype(jnp.bfloat16), "fsdp", scatter_dimension=0, tiled=True
        ).astype(jnp.float32),
    )
    totals = (
        lax.psum(attn_shares[0].astype(jnp.bfloat16), "ctx").astype(jnp.float32),
        lax.psum(attn_shares[1].astype(jnp.bfloat16), "ctx").astype(jnp.float32),
        lax.psum(attn_shares[2].astype(jnp.bfloat16), "ctx").astype(jnp.float32),
        lax.psum(attn_shares[4].astype(jnp.bfloat16), "ctx").astype(jnp.float32),
        lax.psum(attn_shares[5].astype(jnp.bfloat16), "ctx").astype(jnp.float32),
        lax.psum(attn_shares[6].astype(jnp.bfloat16), "ctx").astype(jnp.float32),
        lax.psum(attn_shares[7].astype(jnp.bfloat16), "ctx").astype(jnp.float32),
        lax.psum(attn_shares[3].astype(jnp.bfloat16), "ctx").astype(jnp.float32),
        lax.psum(grad_gate.astype(jnp.bfloat16), "ctx").astype(jnp.float32),
        lax.psum(grad_up.astype(jnp.bfloat16), "ctx").astype(jnp.float32),
        lax.psum(grad_down.astype(jnp.bfloat16), "ctx").astype(jnp.float32),
    )
    return (
        result[None],
        input_grad[None],
        totals[0],
        totals[1],
        totals[2],
        totals[3],
        totals[4],
        totals[5],
        totals[6],
        totals[7],
        totals[8],
        totals[9],
        totals[10],
    )


def solution(mesh):
    return jax.shard_map(
        shards,
        mesh=mesh,
        in_specs=(
            P("fsdp", "ctx", None),
            P("fsdp", "ctx"),
            P(),
            P("fsdp"),
            P("fsdp"),
            P("fsdp"),
            P("fsdp", None),
            P("fsdp", None),
            P("fsdp", None),
            P("fsdp", None),
            P("fsdp"),
            P("fsdp", None),
            P("fsdp", None),
            P("fsdp", None),
            P("fsdp", "ctx", None),
        ),
        out_specs=(
            P("fsdp", "ctx", None),
            P("fsdp", "ctx", None),
            P("fsdp"),
            P("fsdp"),
            P("fsdp"),
            P("fsdp", None),
            P("fsdp", None),
            P("fsdp", None),
            P("fsdp", None),
            P("fsdp"),
            P("fsdp", None),
            P("fsdp", None),
            P("fsdp", None),
        ),
        check_vma=False,
    )
```

profile of v0, /device:TPU:0, one launch (start us, length us, event | category | flops | bytes accessed | tf_op | source)
XLA Modules:
  0.0 1124.8 jit_solution(12885945972591466999)
XLA Ops:
  8.7 13.6 %all-gather = bf16[8,1,128]{2,1,0:T(2,128)(2,1)S(1)} all-gather(bf16[1,1,128]{2,1,0:T(2,128)(2,1)} %bitcast.207), channel_id=1, replica_groups=mesh['ctx'=4,'fsdp'=8] {'fsdp'}, dimensions={0}, use_global_device_ids=true | all-gather | bytes 2304 | tf_op jit(solution)/shard_map/all_gather | solution.py:105
  23.6 11.0 all-gather.12.cloned.1.call-done
  34.6 2.6 convolution_convert_fusion.8
  41.5 15.9 %all-reduce.7 = (bf16[64]{0:T(256)(128)(2,1)S(1)}, bf16[64]{0:T(256)(128)(2,1)S(1)}) all-reduce(bf16[64]{0:T(256)(128)(2,1)S(1)} %dynamic-update-slice, bf16[64]{0:T(256)(128)(2,1)S(1)} %dynamic-update-slice.1), channel_id=1, replica_groups=mesh['ctx'=4,'fsdp'=8] {'fsdp'}, use_global_device_ids=true, to_apply=%add | all-reduce | flops 128 | bytes 512
  64.3 10.6 all-gather.1
  75.3 11.2 all-gather.14.cloned.1.call-done
  88.0 29.1 %all-gather.20.cloned.1.call-done = bf16[1024,1024]{1,0:T(8,128)(2,1)} async-done(((bf16[128,1024]{1,0:T(8,128)(2,1)}), bf16[1024,1024]{1,0:T(8,128)(2,1)}) %all-gather.20.cloned.1.call-update) | async-done | bytes 2097168 | tf_op jit(solution)/shard_map/all_gather | solution.py:109
  117.1 3.9 copy.56
  121.0 2.4 multiply_reduce_fusion.5
  123.9 21.2 %all-gather.18.cloned.1.call-done = bf16[1024,512]{0,1:T(8,128)(2,1)} async-done(((bf16[256,512]{0,1:T(8,128)(2,1)}), bf16[1024,512]{0,1:T(8,128)(2,1)}) %all-gather.18.cloned.1.call-update) | async-done | bytes 1048592 | tf_op jit(solution)/shard_map/all_gather | solution.py:130
  145.1 8.6 fusion.62
  153.8 8.2 fusion.3
  162.0 7.5 fusion.20
  169.5 6.3 all-gather.22.cloned.1.call-done
  175.8 2.4 multiply_reduce_fusion.4
  178.4 89.2 %all-gather.26.cloned.1.call-done = bf16[1024,4608]{1,0:T(8,128)(2,1)} async-done(((bf16[128,4608]{1,0:T(8,128)(2,1)}), bf16[1024,4608]{1,0:T(8,128)(2,1)}) %all-gather.26.cloned.1.call-update) | async-done | bytes 9437200 | tf_op jit(solution)/shard_map/all_gather | solution.py:161
  267.6 7.9 fusion.64
  275.5 82.9 %all-gather.24.cloned.1.call-done = bf16[1024,4608]{1,0:T(8,128)(2,1)} async-done(((bf16[128,4608]{1,0:T(8,128)(2,1)}), bf16[1024,4608]{1,0:T(8,128)(2,1)}) %all-gather.24.cloned.1.call-update) | async-done | bytes 9437200 | tf_op jit(solution)/shard_map/all_gather | solution.py:160
  358.3 8.0 fusion.63
  366.3 82.8 %all-gather.28.cloned.1.call-done = bf16[4608,1024]{1,0:T(8,128)(2,1)} async-done(((bf16[576,1024]{1,0:T(8,128)(2,1)}), bf16[4608,1024]{1,0:T(8,128)(2,1)}) %all-gather.28.cloned.1.call-update) | async-done | bytes 9437200 | tf_op jit(solution)/shard_map/all_gather | solution.py:162
  449.2 13.7 %multiply_convert_fusion = (bf16[256,4608]{1,0:T(8,128)(2,1)S(1)}, bf16[256,4608]{1,0:T(8,128)(2,1)S(1)}, bf16[256,4608]{1,0:T(8,128)(2,1)}) fusion(f32[256,4608]{1,0:T(8,128)} %fusion.63, f32[256,4608]{1,0:T(8,128)} %fusion.64, bf16[4608,1024]{1,0:T(8,128)(2,1)} %all-gather.28.cloned.1.call-done, bf16[1,256,1024]{2,1,0:T(8,128)(2,1)S(1)} %copy-done.18), kind=kOutput, calls=%fused_computation.17 | convolution fusion | flops 2433613824 | bytes 26476544 | tf_op jit(solution)/shard_map/dot_general | solution.py:22
  462.8 2.6 fusion.65
  465.5 6.2 multiply_reduce_fusion
  475.7 9.8 bitcast_convert_fusion
  485.5 11.0 fusion
  496.6 12.2 %fusion.2 = bf16[8,2,256,1024]{2,3,1,0:T(8,128)(2,1)S(1)} fusion(f32[8,1024,256,2]{2,1,3,0:T(8,128)} %get-tuple-element.64, f32[8,2,256,1024]{2,3,1,0:T(8,128)} %get-tuple-element.59, f32[8,2,256]{2,1,0:T(2,128)S(1)} %get-tuple-element.63, f32[8,2,256]{2,1,0:T(2,128)S(1)} %bitcast.191), kind=kLoop, calls=%fused_computation.4 | loop fusion | flops 16777216 | bytes 41975808 | tf_op jit(solution)/shard_map/convert_element_type | solution.py:213
  508.8 3.6 fusion.10
  512.5 10.5 reduce-scatter.12.cloned.1.call-done
  523.0 2.5 convolution_convert_fusion.5
  525.6 28.3 %reduce-scatter.10.cloned.1.call-done = bf16[256,512]{0,1:T(8,128)(2,1)} async-done(((bf16[1024,512]{0,1:T(8,128)(2,1)}), bf16[256,512]{0,1:T(8,128)(2,1)}) %reduce-scatter.10.cloned.1.call-update) | async-done | bytes 262160 | tf_op jit(solution)/shard_map/reduce_scatter | solution.py:227
  559.1 3.2 convolution_convert_fusion.3
  562.4 5.3 convolution_multiply_fusion
  569.4 2.2 convolution_convert_fusion.4
  571.6 8.1 convolution_convert_fusion
  579.8 6.8 convolution_convert_fusion.1
  586.6 7.1 convolution_convert_fusion.2
  593.8 27.9 %reduce-scatter.16.cloned.1.call-done = bf16[128,512]{1,0:T(8,128)(2,1)} async-done(((bf16[1024,512]{1,0:T(8,128)(2,1)}), bf16[128,512]{1,0:T(8,128)(2,1)}) %reduce-scatter.16.cloned.1.call-update) | async-done | bytes 131088 | tf_op jit(solution)/shard_map/reduce_scatter | solution.py:291
  621.7 36.4 %reduce-scatter.20.cloned.1.call-done = bf16[128,1024]{1,0:T(8,128)(2,1)} async-done(((bf16[1024,1024]{1,0:T(8,128)(2,1)}), bf16[128,1024]{1,0:T(8,128)(2,1)}) %reduce-scatter.20.cloned.1.call-update) | async-done | bytes 262160 | tf_op jit(solution)/shard_map/reduce_scatter | solution.py:297
  658.1 36.8 %reduce-scatter.14.cloned.1.call-done = bf16[128,1024]{1,0:T(8,128)(2,1)} async-done(((bf16[1024,1024]{1,0:T(8,128)(2,1)}), bf16[128,1024]{1,0:T(8,128)(2,1)}) %reduce-scatter.14.cloned.1.call-update) | async-done | bytes 262160 | tf_op jit(solution)/shard_map/reduce_scatter | solution.py:288
  695.0 100.2 %reduce-scatter.26.cloned.1.call-done = bf16[576,1024]{1,0:T(8,128)(2,1)} async-done(((bf16[4608,1024]{1,0:T(8,128)(2,1)}), bf16[576,1024]{1,0:T(8,128)(2,1)}) %reduce-scatter.26.cloned.1.call-update) | async-done | bytes 1179664 | tf_op jit(solution)/shard_map/reduce_scatter | solution.py:185
  795.2 100.1 %reduce-scatter.24.cloned.1.call-done = bf16[128,4608]{1,0:T(8,128)(2,1)} async-done(((bf16[1024,4608]{1,0:T(8,128)(2,1)}), bf16[128,4608]{1,0:T(8,128)(2,1)}) %reduce-scatter.24.cloned.1.call-update) | async-done | bytes 1179664 | tf_op jit(solution)/shard_map/reduce_scatter | solution.py:182
  895.2 100.1 %reduce-scatter.22.cloned.1.call-done = bf16[128,4608]{1,0:T(8,128)(2,1)} async-done(((bf16[1024,4608]{1,0:T(8,128)(2,1)}), bf16[128,4608]{1,0:T(8,128)(2,1)}) %reduce-scatter.22.cloned.1.call-update) | async-done | bytes 1179664 | tf_op jit(solution)/shard_map/reduce_scatter | solution.py:179
  996.7 2.3 fusion.66
  999.0 7.9 fusion.21
  1008.2 13.9 %all-reduce.6 = (bf16[1024]{0:T(1024)(128)(2,1)S(1)}, bf16[64]{0:T(256)(128)(2,1)S(1)}, bf16[64]{0:T(256)(128)(2,1)S(1)}, bf16[1024]{0:T(1024)(128)(2,1)S(1)}) all-reduce(bf16[1024]{0:T(1024)(128)(2,1)S(1)} %get-tuple-element.17, bf16[64]{0:T(256)(128)(2,1)S(1)} %get-tuple-element.13, ...), channel_id=4, replica_groups=mesh['ctx'=4,'fsdp'=8] {'fsdp'}, use_global_device_ids=true, to_apply=%region_15.16.clone | all-reduce | flops 2176 | bytes 8704
  1022.5 10.0 all-reduce.8
  1035.6 69.2 %all-reduce.12.cloned.1.call-done = (bf16[128,1024]{1,0:T(8,128)(2,1)}, bf16[128,512]{1,0:T(8,128)(2,1)}, bf16[128,512]{1,0:T(8,128)(2,1)}, bf16[128,1024]{1,0:T...) async-done(((bf16[128,1024]{1,0:T(8,128)(2,1)}, bf16[128,512]{1,0:T(8,128)(2,1)}, bf16[128,512]{1,0:T(8,128)(2,1)}, ...) | async-done | bytes 4325392 | tf_op jit(solution)/shard_map/psum | solution.py:305
  1111.8 2.9 convert_element_type.285
  (158 shorter events, 41.9 us)
Async XLA Ops:
  7.2 52.7 %copy-start.1 = (bf16[1,256,1024]{2,1,0:T(8,128)(2,1)S(1)}, bf16[1,256,1024]{2,1,0:T(8,128)(2,1)}, u32[]{:S(2)}) copy-start(bf16[1,256,1024]{2,1,0:T(8,128)(2,1)} %param.15) | copy-start | bytes 1572868
  7.2 27.4 %all-gather.12.cloned.1.call-start = ((), (), s32[]{:S(2)}) async-start(), calls=%async_computation.9 | async-start | bytes 1179648 | tf_op jit(solution)/shard_map/all_gather | solution.py:111
  7.9 50.4 %all-gather.16.cloned.1.call-start = ((), (), s32[]{:S(2)}) async-start(), calls=%async_computation.11 | async-start | bytes 1179648 | tf_op jit(solution)/shard_map/all_gather | solution.py:110
  8.7 77.8 %all-gather.14.cloned.1.call-start = ((), (), s32[]{:S(2)}) async-start(), calls=%async_computation.10 | async-start | bytes 1310720 | tf_op jit(solution)/shard_map/all_gather | solution.py:131
  37.2 79.9 %all-gather.20.cloned.1.call-start = ((), (), s32[]{:S(2)}) async-start(), calls=%async_computation.13 | async-start | bytes 2359296 | tf_op jit(solution)/shard_map/all_gather | solution.py:109
  37.8 107.4 %all-gather.18.cloned.1.call-start = ((), (), s32[]{:S(2)}) async-start(), calls=%async_computation.12 | async-start | bytes 1310720 | tf_op jit(solution)/shard_map/all_gather | solution.py:130
  59.8 4.4 copy-start.25
  59.9 15.0 %copy-start.26 = (s32[4]{0:T(128)S(1)}, s32[4]{0:T(128)}, u32[]{:S(2)}) copy-start(s32[4]{0:T(128)} %param.17) | copy-start | bytes 52
  60.5 60.6 %copy-start.7 = (f32[256,8,64]{0,2,1:T(8,128)}, f32[256,8,64]{0,2,1:T(8,128)S(1)}, u32[]{:S(2)}) copy-start(f32[256,8,64]{0,2,1:T(8,128)S(1)} %get-tuple-element.55) | copy-start | bytes 1572868
  61.4 114.4 %all-gather.22.cloned.1.call-start = ((), (), s32[]{:S(2)}) async-start(), calls=%async_computation.14 | async-start | bytes 2359296 | tf_op jit(solution)/shard_map/all_gather | solution.py:112
  62.0 205.6 %all-gather.26.cloned.1.call-start = ((), (), s32[]{:S(2)}) async-start(), calls=%async_computation.16 | async-start | bytes 10616832 | tf_op jit(solution)/shard_map/all_gather | solution.py:161
  62.7 295.6 %all-gather.24.cloned.1.call-start = ((), (), s32[]{:S(2)}) async-start(), calls=%async_computation.15 | async-start | bytes 10616832 | tf_op jit(solution)/shard_map/all_gather | solution.py:160
  63.5 385.7 %all-gather.28.cloned.1.call-start = ((), (), s32[]{:S(2)}) async-start(), calls=%async_computation.17 | async-start | bytes 10616832 | tf_op jit(solution)/shard_map/all_gather | solution.py:162
  64.2 458.8 %reduce-scatter.12.cloned.1.call-start = ((), (), s32[]{:S(2)}) async-start(), calls=%async_computation.19 | async-start | bytes 1310720 | tf_op jit(solution)/shard_map/reduce_scatter | solution.py:233
  88.0 74.0 %copy-start.10 = (bf16[1024,512]{0,1:T(8,128)(2,1)}, bf16[1024,512]{0,1:T(8,128)(2,1)S(1)}, u32[]{:S(2)}) copy-start(bf16[1024,512]{0,1:T(8,128)(2,1)S(1)} %copy.54) | copy-start | bytes 3145732
  123.5 30.3 %copy-start.3 = (f32[256,16,64]{0,2,1:T(8,128)}, f32[256,16,64]{0,2,1:T(8,128)S(1)}, u32[]{:S(2)}) copy-start(f32[256,16,64]{0,2,1:T(8,128)S(1)} %get-tuple-element.57) | copy-start | bytes 3145732
  123.9 29.9 %copy-start.13 = (bf16[256,16,32]{0,2,1:T(8,128)(2,1)}, bf16[256,16,32]{0,2,1:T(8,128)(2,1)S(1)}, u32[]{:S(2)}) copy-start(bf16[256,16,32]{0,2,1:T(8,128)(2,1)S(1)} %get-tuple-element.44) | copy-start | bytes 786436
  169.5 106.0 %copy-start.17 = (bf16[8,64,2,256]{3,1,2,0:T(8,128)(2,1)}, bf16[8,64,2,256]{3,1,2,0:T(8,128)(2,1)S(1)}, u32[]{:S(2)}) copy-start(bf16[8,64,2,256]{3,1,2,0:T(8,128)(2,1)S(1)} %fusion.20) | copy-start | bytes 1572868
  275.5 173.7 %copy-start.18 = (bf16[1,256,1024]{2,1,0:T(8,128)(2,1)S(1)}, bf16[1,256,1024]{2,1,0:T(8,128)(2,1)}, u32[]{:S(2)}) copy-start(bf16[1,256,1024]{2,1,0:T(8,128)(2,1)} %param.29) | copy-start | bytes 1572868
  449.2 13.7 %copy-start.2 = (bf16[1024,4608]{1,0:T(8,128)(2,1)S(1)}, bf16[1024,4608]{1,0:T(8,128)(2,1)}, u32[]{:S(2)}) copy-start(bf16[1024,4608]{1,0:T(8,128)(2,1)} %all-gather.24.cloned.1.call-done) | copy-start | bytes 28311556
  462.8 2.6 copy-start.15
  462.8 2.6 copy-start.16
  465.5 6.2 copy-start.19
  465.5 6.5 copy-start.5
  475.7 9.8 copy-start.6
  475.7 9.8 copy-start.11
  496.5 57.4 %reduce-scatter.10.cloned.1.call-start = ((), (), s32[]{:S(2)}) async-start(), calls=%async_computation.18 | async-start | bytes 1310720 | tf_op jit(solution)/shard_map/reduce_scatter | solution.py:227
  496.5 12.3 %copy-start.14 = (bf16[256,16,32]{0,2,1:T(8,128)(2,1)S(1)}, bf16[256,16,32]{0,2,1:T(8,128)(2,1)}, u32[]{:S(2)}) copy-start(bf16[256,16,32]{0,2,1:T(8,128)(2,1)} %copy-done.13) | copy-start | bytes 786436
  508.8 3.6 copy-start
  512.4 81.4 %reduce-scatter.18.cloned.1.call-start = ((), (), s32[]{:S(2)}) async-start(), calls=%async_computation.22 | async-start | bytes 1179648 | tf_op jit(solution)/shard_map/reduce_scatter | solution.py:294
  525.6 96.1 %reduce-scatter.16.cloned.1.call-start = ((), (), s32[]{:S(2)}) async-start(), calls=%async_computation.21 | async-start | bytes 1179648 | tf_op jit(solution)/shard_map/reduce_scatter | solution.py:291
  559.1 99.1 %reduce-scatter.20.cloned.1.call-start = ((), (), s32[]{:S(2)}) async-start(), calls=%async_computation.23 | async-start | bytes 2359296 | tf_op jit(solution)/shard_map/reduce_scatter | solution.py:297
  562.4 132.6 %reduce-scatter.14.cloned.1.call-start = ((), (), s32[]{:S(2)}) async-start(), calls=%async_computation.20 | async-start | bytes 2359296 | tf_op jit(solution)/shard_map/reduce_scatter | solution.py:288
  562.4 5.5 copy-start.4
  568.6 0.8 copy-start.8
  571.6 223.6 %reduce-scatter.26.cloned.1.call-start = ((), (), s32[]{:S(2)}) async-start(), calls=%async_computation.26 | async-start | bytes 10616832 | tf_op jit(solution)/shard_map/reduce_scatter | solution.py:185
  579.7 315.5 %reduce-scatter.24.cloned.1.call-start = ((), (), s32[]{:S(2)}) async-start(), calls=%async_computation.25 | async-start | bytes 10616832 | tf_op jit(solution)/shard_map/reduce_scatter | solution.py:182
  586.6 408.7 %reduce-scatter.22.cloned.1.call-start = ((), (), s32[]{:S(2)}) async-start(), calls=%async_computation.24 | async-start | bytes 10616832 | tf_op jit(solution)/shard_map/reduce_scatter | solution.py:179
  593.7 402.9 %copy-start.9 = (bf16[256,16,64]{0,2,1:T(8,128)(2,1)S(1)}, bf16[256,16,64]{0,2,1:T(8,128)(2,1)}, u32[]{:S(2)}) copy-start(bf16[256,16,64]{0,2,1:T(8,128)(2,1)} %copy-done.8) | copy-start | bytes 1572868
  593.8 511.0 %all-reduce.12.cloned.1.call-start = ((), (), s32[]{:S(2)}) async-start(), calls=%async_computation.27 | async-start | bytes 8650752 | tf_op jit(solution)/shard_map/psum | solution.py:305
  999.0 8.0 copy-start.12
  999.0 8.5 copy-start.22
  999.0 8.5 copy-start.23
  1007.0 1.3 copy-start.24
  1104.8 9.9 copy-start.21
  1104.8 11.6 %copy-start.20 = (bf16[576,1024]{1,0:T(8,128)(2,1)S(1)}, bf16[576,1024]{1,0:T(8,128)(2,1)}, u32[]{:S(2)}) copy-start(bf16[576,1024]{1,0:T(8,128)(2,1)} %get-tuple-element.37) | copy-start | bytes 3538948
Sparse Core Ops, SparseCore 0:
  9.6 24.9 all-gather.11
  36.2 21.9 all-gather.15
  60.6 25.8 all-gather.13
  87.9 29.1 all-gather.19
  119.3 25.7 all-gather.17
  146.6 29.1 all-gather.21
  177.4 90.0 all-gather.25
  269.2 89.1 all-gather.23
  360.0 89.1 all-gather.27
  496.6 26.3 reduce-scatter.11
  525.9 27.9 reduce-scatter.9
  556.0 32.5 reduce-scatter.17
  590.9 30.7 reduce-scatter.15
  623.9 34.2 reduce-scatter.19
  660.3 34.6 reduce-scatter.13
  697.1 97.9 reduce-scatter.25
  797.3 97.8 reduce-scatter.23
  897.4 97.8 reduce-scatter.21
  999.9 104.8 all-reduce.11
where the time goes:
time: 1130 us; the launch traced here: 1120 us
  waiting for transfers between devices  848 us (75%)
  matrix products  137 us (12%)
  blocking collectives  64 us (6%)
  other arithmetic  45.4 us (4%)
  between operations  16.8 us (1%)
  local copies, waits for them, and re-layouts  13.3 us (1%)
    reduce_scatter x1, waiting for transfers between devices, shards(): lax.psum_scatter(local_down.astype(jnp.bfloat16), 'fsdp', scatter_dimensi...  100 us
    reduce_scatter x1, waiting for transfers between devices, shards(): lax.psum_scatter(local_gate.astype(jnp.bfloat16), 'fsdp', scatter_dimensi...  100 us
    reduce_scatter x1, waiting for transfers between devices, shards(): lax.psum_scatter(local_up.astype(jnp.bfloat16), 'fsdp', scatter_dimension...  100 us
    all_gather x1, waiting for transfers between devices, shards(): lax.all_gather(up_weight, 'fsdp', axis=0, tiled=True)  89.2 us
    all_gather x1, waiting for transfers between devices, shards(): lax.all_gather(gate_weight, 'fsdp', axis=0, tiled=True)  82.9 us
    all_gather x1, waiting for transfers between devices, shards(): lax.all_gather(down_weight, 'fsdp', axis=0, tiled=True)  82.8 us
    psum x1, waiting for transfers between devices, shards(): lax.psum(attn_shares[4].astype(jnp.bfloat16), 'ctx').astype(jnp.float32)  69.2 us
    reduce_scatter x1, waiting for transfers between devices, shards(): lax.psum_scatter(grad_query.astype(jnp.bfloat16), 'fsdp', scatter_dimensi...  36.8 us
  transfers between devices with their start and end apart: 19, of which 17 were waited for; matrix products, arithmetic and copies ran while one was open for 12% of the time, Pallas kernels for 0%

commit v1 on v0

v1 whole, which is shorter than its diff:
```python
import functools

import jax
import jax.numpy as jnp
from jax import lax
from jax.experimental import pallas as pl
from jax.experimental.pallas import tpu as pltpu
from jax.sharding import PartitionSpec as P


H = 16
HD = 64
KV = 8
GROUPS = H // KV

epsilon = 1e-05
theta_base = 1000000.0
score_scale = 0.125
masked_value = -1e30


def dot_plain(left, right):
    return jnp.dot(left, right, preferred_element_type=jnp.float32)


def times_transposed(left, right):
    return lax.dot_general(
        left, right, (((1,), (1,)), ((), ())), preferred_element_type=jnp.float32
    )


def transposed_times(left, right):
    return lax.dot_general(
        left, right, (((0,), (0,)), ((), ())), preferred_element_type=jnp.float32
    )


def exact_dot(left, right):
    return jnp.dot(
        left, right, preferred_element_type=jnp.float32, precision=lax.Precision.HIGHEST
    )


def unit_norm(values):
    inverse = lax.rsqrt(jnp.mean(values * values, axis=-1, keepdims=True) + epsilon)
    return values * inverse, inverse


def norm_backward(scaled, normal, inverse):
    inner = jnp.mean(scaled * normal, axis=-1, keepdims=True)
    return inverse * (scaled - normal * inner)


def lane_tables(width):
    row = lax.broadcasted_iota(jnp.int32, (width, width), 0)
    col = lax.broadcasted_iota(jnp.int32, (width, width), 1)
    mean = jnp.where(row // HD == col // HD, 1.0 / HD, 0.0).astype(jnp.float32)
    low = col % HD < HD // 2
    partner = jnp.where(low, col + HD // 2, col - HD // 2)
    swap = jnp.where(row == partner, 1.0, 0.0).astype(jnp.float32)
    lane = lax.broadcasted_iota(jnp.int32, (1, width), 1)
    sign = jnp.where(lane % HD < HD // 2, -1.0, 1.0).astype(jnp.float32)
    return mean, swap, sign


def chunk_widths(width):
    step = min(width, 2 * HD)
    return [(start, step) for start in range(0, width, step)]


def attention_forward_kernel(
    qkv_ref, cos_ref, sin_ref, gq_ref, gk_ref, ob_ref, qs_ref, ks_ref, vs_ref, os_ref,
    *, q_width, kv_width, rows, block
):
    q_heads = q_width // HD
    kv_heads = kv_width // HD
    for base, width, gain_ref, out_ref, scale in (
        (0, q_width, gq_ref, qs_ref, score_scale),
        (q_width, kv_width, gk_ref, ks_ref, 1.0),
    ):
        for start, step in chunk_widths(width):
            mean, swap, sign = lane_tables(step)
            for row in range(0, rows, block):
                here = pl.ds(row, block)
                raw = qkv_ref[here, pl.ds(base + start, step)]
                inverse = lax.rsqrt(exact_dot(raw * raw, mean) + epsilon)
                normed = raw * inverse * gain_ref[:, :step]
                turned = normed * cos_ref[here, :step] + exact_dot(normed, swap) * (
                    sin_ref[here, :step] * sign
                )
                low = turned.astype(jnp.bfloat16) * jnp.bfloat16(scale)
                for part in range(step // HD):
                    out_ref[start // HD + part, here, :] = low[:, part * HD : (part + 1) * HD]
    for head in range(kv_heads):
        at = q_width + kv_width + head * HD
        vs_ref[head] = qkv_ref[:, pl.ds(at, HD)].astype(jnp.bfloat16)

    def one_head(head, carry):
        pair = head // GROUPS
        for row in range(0, rows, block):
            upto = row + block
            q_here = qs_ref[head, pl.ds(row, block), :]
            scores = times_transposed(q_here, ks_ref[pair, pl.ds(0, upto), :])
            own = lax.broadcasted_iota(jnp.int32, (block, upto), 0) + row
            other = lax.broadcasted_iota(jnp.int32, (block, upto), 1)
            scores = jnp.where(own >= other, scores, masked_value)
            top = jnp.max(scores, axis=-1, keepdims=True)
            expo = jnp.exp(scores - top)
            probs = (expo * (1.0 / jnp.sum(expo, axis=-1, keepdims=True))).astype(jnp.bfloat16)
            mixed = dot_plain(probs, vs_ref[pair, pl.ds(0, upto), :])
            os_ref[head, pl.ds(row, block), :] = mixed.astype(jnp.bfloat16)
        return carry

    lax.fori_loop(0, q_heads, one_head, 0)
    for head in range(q_heads):
        ob_ref[:, head * HD : (head + 1) * HD] = os_ref[head]


def attention_backward_kernel(
    qkv_ref, cos_ref, sin_ref, gq_ref, gk_ref, qs_ref, ks_ref, vs_ref, dob_ref,
    dqkv_ref, gains_ref, do_ref, dq_ref, dk_ref, dv_ref,
    *, q_width, kv_width, rows, block
):
    q_heads = q_width // HD
    kv_heads = kv_width // HD
    for head in range(q_heads):
        do_ref[head] = dob_ref[:, head * HD : (head + 1) * HD]
    dk_ref[...] = jnp.zeros_like(dk_ref)
    dv_ref[...] = jnp.zeros_like(dv_ref)

    def one_head(head, carry):
        pair = head // GROUPS
        for row in range(0, rows, block):
            upto = row + block
            here = pl.ds(row, block)
            seen = pl.ds(0, upto)
            q_here = qs_ref[head, here, :]
            do_here = do_ref[head, here, :]
            scores = times_transposed(q_here, ks_ref[pair, seen, :])
            own = lax.broadcasted_iota(jnp.int32, (block, upto), 0) + row
            other = lax.broadcasted_iota(jnp.int32, (block, upto), 1)
            scores = jnp.where(own >= other, scores, masked_value)
            top = jnp.max(scores, axis=-1, keepdims=True)
            expo = jnp.exp(scores - top)
            probs = expo * (1.0 / jnp.sum(expo, axis=-1, keepdims=True))
            prob_grad = times_transposed(do_here, vs_ref[pair, seen, :])
            inner = jnp.sum(probs * prob_grad, axis=-1, keepdims=True)
            score_grad = (probs * (prob_grad - inner)).astype(jnp.bfloat16)
            dq_ref[head, here, :] = dot_plain(score_grad, ks_ref[pair, seen, :]) * score_scale
            dk_ref[pair, seen, :] += transposed_times(score_grad, q_here)
            dv_ref[pair, seen, :] += transposed_times(probs.astype(jnp.bfloat16), do_here)
        return carry

    lax.fori_loop(0, q_heads, one_head, 0)
    gains_ref[...] = jnp.zeros_like(gains_ref)
    for slot, base, width, gain_ref, grad_ref in (
        (0, 0, q_width, gq_ref, dq_ref),
        (1, q_width, kv_width, gk_ref, dk_ref),
    ):
        for start, step in chunk_widths(width):
            mean, swap, sign = lane_tables(step)
            for row in range(0, rows, block):
                here = pl.ds(row, block)
                first = start // HD
                turned = jnp.concatenate(
                    [grad_ref[first + part, here, :] for part in range(step // HD)], axis=1
                )
                normed_grad = turned * cos_ref[here, :step] - exact_dot(turned, swap) * (
                    sin_ref[here, :step] * sign
                )
                raw = qkv_ref[here, pl.ds(base + start, step)]
                inverse = lax.rsqrt(exact_dot(raw * raw, mean) + epsilon)
                unit = raw * inverse
                gains_ref[slot : slot + 1, :step] += jnp.sum(
                    normed_grad * unit, axis=0, keepdims=True
                )
                scaled = normed_grad * gain_ref[:, :step]
                raw_grad = inverse * (scaled - unit * exact_dot(scaled * unit, mean))
                dqkv_ref[here, pl.ds(base + start, step)] = raw_grad.astype(jnp.bfloat16)
    for head in range(kv_heads):
        at = q_width + kv_width + head * HD
        dqkv_ref[:, at : at + HD] = dv_ref[head].astype(jnp.bfloat16)


def spread_kernel(parts_ref, gate_ref, up_ref, *, shards_of, ranks, piece):
    half = shards_of * piece
    for base, out_ref in ((0, gate_ref), (half, up_ref)):
        out_ref[...] = jnp.concatenate(
            [
                parts_ref[rank, :, base + shard * piece : base + (shard + 1) * piece]
                for shard in range(shards_of)
                for rank in range(ranks)
            ],
            axis=1,
        ).astype(jnp.float32)


def pick_kernel(rank_ref, gate_ref, up_ref, out_ref, *, shards_of, ranks, piece):
    half = shards_of * piece
    for rank in range(ranks):

        @pl.when(rank_ref[0] == rank)
        def _():
            for base, in_ref in ((0, gate_ref), (half, up_ref)):
                out_ref[:, base : base + half] = jnp.concatenate(
                    [
                        in_ref[:, (shard * ranks + rank) * piece : (shard * ranks + rank + 1) * piece]
                        for shard in range(shards_of)
                    ],
                    axis=1,
                )


def call_kernel(kernel, out_shapes, scratch=(), smem_first=False, count=0):
    vmem = pl.BlockSpec(memory_space=pltpu.VMEM)
    in_specs = [vmem] * count
    if smem_first:
        in_specs[0] = pl.BlockSpec(memory_space=pltpu.SMEM)
    return pl.pallas_call(
        kernel,
        out_shape=out_shapes,
        in_specs=in_specs,
        out_specs=jax.tree.map(lambda _: vmem, out_shapes),
        scratch_shapes=scratch,
        compiler_params=pltpu.CompilerParams(vmem_limit_bytes=56 * 1024 * 1024),
    )


def shards(
    tokens,
    positions,
    block_pairs,
    input_gain,
    query_gain,
    key_gain,
    query_weight,
    key_weight,
    value_weight,
    out_weight,
    middle_gain,
    gate_weight,
    up_weight,
    down_weight,
    cotangent,
):
    ranks = lax.axis_size("ctx")
    owners = lax.axis_size("fsdp")
    me = lax.axis_index("ctx")
    own_tokens = tokens[0]
    rows_here, model = own_tokens.shape
    half_rows = rows_here // 2
    rows = rows_here * ranks
    others = range(1, ranks)
    bf16 = jnp.bfloat16
    f32 = jnp.float32
    q_width = H // ranks * HD
    kv_width = KV // ranks * HD
    width = q_width + 2 * kv_width
    model_part = model // owners
    hidden_width = gate_weight.shape[1]
    piece = hidden_width // (owners * ranks)
    hidden_here = owners * piece

    def send(value, step):
        return lax.ppermute(value, "ctx", [(i, i ^ step) for i in range(ranks)])

    def gather_ctx(value):
        return [value] + [send(value, step) for step in others]

    def by_rank(parts):
        stack = jnp.zeros((ranks,) + parts[0].shape, parts[0].dtype)
        for step, part in enumerate(parts):
            stack = lax.dynamic_update_index_in_dim(stack, part, me ^ step, 0)
        return stack

    place = lax.axis_index("fsdp")
    core = place % 2
    chip = place // 2
    chips = owners // 2

    def send_owner(value, step):
        return lax.ppermute(value, "fsdp", [(i, i ^ step) for i in range(owners)])

    def gather_owners(value):
        stack = jnp.zeros((chips,) + value.shape, value.dtype)
        for step in range(chips):
            part = send_owner(value, 2 * step) if step else value
            stack = lax.dynamic_update_index_in_dim(stack, part, chip ^ step, 0)
        partner = send_owner(stack, 1)
        first = jnp.where(core == 0, stack, partner)
        second = jnp.where(core == 0, partner, stack)
        return jnp.stack([first, second], axis=1)

    def scatter_owners(value):
        mine = jnp.where(core == 0, value[:, 0], value[:, 1])
        theirs = send_owner(jnp.where(core == 0, value[:, 1], value[:, 0]), 1)
        pair = (mine.astype(f32) + theirs.astype(f32)).astype(bf16)
        total = lax.dynamic_index_in_dim(pair, chip, 0, keepdims=False).astype(f32)
        for step in range(1, chips):
            entry = lax.dynamic_index_in_dim(pair, chip ^ step, 0, keepdims=False)
            total = total + send_owner(entry, 2 * step).astype(f32)
        return total.astype(bf16)

    hold = lax.optimization_barrier

    def block_starts(step):
        low = lax.dynamic_index_in_dim(block_pairs, me ^ step, 0, keepdims=False)
        return low * half_rows, (2 * ranks - 1 - low) * half_rows

    def true_order(parts):
        out = jnp.zeros((rows,) + parts[0].shape[1:], parts[0].dtype)
        for step, part in enumerate(parts):
            low, high = block_starts(step)
            out = lax.dynamic_update_slice_in_dim(out, part[:half_rows], low, 0)
            out = lax.dynamic_update_slice_in_dim(out, part[half_rows:], high, 0)
        return out

    def rows_of(value, step):
        low, high = block_starts(step)
        return jnp.concatenate(
            [
                lax.dynamic_slice_in_dim(value, low, half_rows, 0),
                lax.dynamic_slice_in_dim(value, high, half_rows, 0),
            ],
            axis=0,
        )

    def columns(weight, size):
        return lax.dynamic_slice_in_dim(weight, me * size, size, 1)

    def gain_row(gain):
        return jnp.pad(gain, (0, width - gain.shape[0]))[None]

    attn_pack = jnp.concatenate(
        [
            columns(query_weight, q_width),
            columns(key_weight, kv_width),
            columns(value_weight, kv_width),
        ],
        axis=1,
    )
    gain_pack = jnp.concatenate(
        [gain_row(g) for g in (input_gain, middle_gain, query_gain, key_gain)]
        + [jnp.zeros((12, width), bf16)],
        axis=0,
    )
    token_parts = gather_ctx(own_tokens)
    place_parts = gather_ctx(positions[0])
    attn_all = gather_owners(
        jnp.concatenate([attn_pack, gain_pack], axis=0)
    ).reshape(owners, model_part + 16, width)
    qkv_weight = attn_all[:, :model_part].reshape(model, width)
    gain_one = attn_all[:, model_part, :model_part].reshape(1, model).astype(f32)
    gain_two = attn_all[:, model_part + 1, :model_part].reshape(1, model).astype(f32)
    head_part = HD // owners
    gain_query = attn_all[:, model_part + 2, :head_part].reshape(1, HD).astype(f32)
    gain_key = attn_all[:, model_part + 3, :head_part].reshape(1, HD).astype(f32)
    gain_query = jnp.tile(gain_query, (1, 2))
    gain_key = jnp.tile(gain_key, (1, 2))
    out_full = lax.all_gather(out_weight, "fsdp", axis=0, tiled=True)
    pick = functools.partial(pick_kernel, shards_of=owners, ranks=ranks, piece=piece)
    wide_pack = call_kernel(
        pick,
        jax.ShapeDtypeStruct((model_part, 2 * hidden_here), bf16),
        smem_first=True,
        count=3,
    )(me.astype(jnp.int32)[None], gate_weight, up_weight)
    wide_all = lax.all_gather(wide_pack, "fsdp", axis=0, tiled=True)
    down_all = lax.all_gather(
        lax.dynamic_slice_in_dim(down_weight, me * piece, piece, 0),
        "fsdp",
        axis=0,
        tiled=True,
    )

    tokens_all = true_order(token_parts)
    upstream = cotangent[0]
    tokens_all, late_upstream = hold((tokens_all, upstream))
    upstream_parts = gather_ctx(late_upstream)
    upstream_all = jnp.concatenate(upstream_parts, axis=0)
    tokens_all = tokens_all.astype(f32)
    places = true_order(place_parts)
    normal_all, _ = unit_norm(tokens_all)
    normed = (normal_all * gain_one).astype(bf16)
    qkv = dot_plain(normed, qkv_weight)
    half_dim = HD // 2
    freqs = theta_base ** (-(jnp.arange(half_dim, dtype=f32) * 2.0) / HD)
    angles = places.astype(f32)[:, None] * jnp.tile(freqs, 4)[None, :]
    cosine = jnp.cos(angles)
    sine = jnp.sin(angles)
    q_heads = q_width // HD
    kv_heads = kv_width // HD
    block = 256
    sizes = dict(q_width=q_width, kv_width=kv_width, rows=rows, block=block)
    mixed_heads, q_low, k_low, v_low = call_kernel(
        functools.partial(attention_forward_kernel, **sizes),
        (
            jax.ShapeDtypeStruct((rows, q_width), bf16),
            jax.ShapeDtypeStruct((q_heads, rows, HD), bf16),
            jax.ShapeDtypeStruct((kv_heads, rows, HD), bf16),
            jax.ShapeDtypeStruct((kv_heads, rows, HD), bf16),
        ),
        scratch=(pltpu.VMEM((q_heads, rows, HD), bf16),),
        count=5,
    )(qkv, cosine, sine, gain_query, gain_key)
    head_parts = [rows_of(mixed_heads, 0)] + [send(rows_of(mixed_heads, s), s) for s in others]
    stacked = by_rank(head_parts)
    mixed = jnp.concatenate([stacked[r] for r in range(ranks)], axis=1)
    middle = own_tokens.astype(f32) + dot_plain(mixed, out_full)

    normal_two, inverse_two = unit_norm(middle)
    normed_two = (normal_two * gain_two).astype(bf16)
    normed_two_all = jnp.concatenate(gather_ctx(normed_two), axis=0)
    gate_all = wide_all[:, :hidden_here]
    up_all = wide_all[:, hidden_here:]
    gate = dot_plain(normed_two_all, gate_all)
    up_values = dot_plain(normed_two_all, up_all)
    sigma = jax.nn.sigmoid(gate)
    swish = gate * sigma
    act = (swish * up_values).astype(bf16)
    down_local = transposed_times(act, upstream_all).astype(bf16)
    down_all, down_local = hold((down_all, down_local))
    down_share = lax.psum_scatter(down_local, "fsdp", scatter_dimension=0, tiled=True)
    act_grad = times_transposed(upstream_all, down_all)
    gate_grad = (act_grad * up_values * sigma * (1.0 + gate * (1.0 - sigma))).astype(bf16)
    up_grad = (act_grad * swish).astype(bf16)

    def part_rows(value, step):
        return value[step * rows_here : (step + 1) * rows_here]

    def wide_back(step):
        return times_transposed(part_rows(gate_grad, step), gate_all) + times_transposed(
            part_rows(up_grad, step), up_all
        )

    back_parts = [send(wide_back(s).astype(bf16), s) for s in others]
    normed_two_grad = wide_back(0)
    wide_local = jnp.concatenate(
        [
            transposed_times(normed_two_all, gate_grad).astype(bf16),
            transposed_times(normed_two_all, up_grad).astype(bf16),
        ],
        axis=1,
    )
    out_partial = dot_plain(act, down_all).astype(bf16)
    back_parts, wide_local, out_partial = hold((back_parts, wide_local, out_partial))
    wide_share = lax.psum_scatter(wide_local, "fsdp", scatter_dimension=0, tiled=True)
    for part in back_parts:
        normed_two_grad = normed_two_grad + part.astype(f32)
    out_parts = [send(part_rows(out_partial, s), s) for s in others]
    middle_grad = upstream.astype(f32) + norm_backward(
        normed_two_grad * gain_two, normal_two, inverse_two
    )
    gain_two_grad = jnp.sum(normed_two_grad * normal_two, axis=0)

    middle_low = middle_grad.astype(bf16)
    mixed_grad = times_transposed(middle_low, out_full).astype(bf16)
    out_local = transposed_times(mixed, middle_low).astype(bf16)
    mixed_grad_parts = []
    for step in range(ranks):
        piece_of = lax.dynamic_slice_in_dim(mixed_grad, (me ^ step) * q_width, q_width, 1)
        mixed_grad_parts.append(send(piece_of, step) if step else piece_of)
    mixed_grad_parts, out_local = hold((mixed_grad_parts, out_local))
    out_share = lax.psum_scatter(out_local, "fsdp", scatter_dimension=0, tiled=True)
    mixed_grad_heads = true_order(mixed_grad_parts)
    qkv_grad, head_gain_grads = call_kernel(
        functools.partial(attention_backward_kernel, **sizes),
        (
            jax.ShapeDtypeStruct((rows, width), bf16),
            jax.ShapeDtypeStruct((8, 2 * HD), f32),
        ),
        scratch=(
            pltpu.VMEM((q_heads, rows, HD), bf16),
            pltpu.VMEM((q_heads, rows, HD), f32),
            pltpu.VMEM((kv_heads, rows, HD), f32),
            pltpu.VMEM((kv_heads, rows, HD), f32),
        ),
        count=9,
    )(qkv, cosine, sine, gain_query, gain_key, q_low, k_low, v_low, mixed_grad_heads)
    out_parts, late_middle, own_partial, _ = hold(
        (out_parts, middle, part_rows(out_partial, 0), qkv_grad)
    )
    result = late_middle + own_partial.astype(f32)
    for part in out_parts:
        result = result + part.astype(f32)
    result = result.astype(bf16)
    normed_grad = times_transposed(qkv_grad, qkv_weight)
    gain_one_grad = jnp.sum(normed_grad * normal_all, axis=0)
    normed_grad_low = normed_grad.astype(bf16)
    own_grad = rows_of(normed_grad_low, 0).astype(f32)
    own_parts = [send(rows_of(normed_grad_low, step), step) for step in others]
    for part in own_parts:
        own_grad = own_grad + part.astype(f32)
    normal_own, inverse_own = unit_norm(own_tokens.astype(f32))
    input_grad = (
        middle_grad + norm_backward(own_grad * gain_one, normal_own, inverse_own)
    ).astype(bf16)

    head_gains = head_gain_grads[:2, :HD] + head_gain_grads[:2, HD:]

    def gain_rows(grad, size):
        return jnp.pad(grad.reshape(owners, size), ((0, 0), (0, width - size)))

    gain_block = jnp.stack(
        [
            gain_rows(gain_one_grad, model_part),
            gain_rows(gain_two_grad, model_part),
            gain_rows(head_gains[0], head_part),
            gain_rows(head_gains[1], head_part),
        ],
        axis=1,
    )
    gain_block = hold(jnp.pad(gain_block.astype(bf16), ((0, 0), (0, 12), (0, 0))))
    weight_block = transposed_times(normed, qkv_grad).astype(bf16)
    grad_pack = jnp.concatenate(
        [weight_block.reshape(owners, model_part, width), gain_block], axis=1
    )
    attn_share = scatter_owners(grad_pack.reshape(chips, 2, model_part + 16, width))

    down_stack = by_rank(gather_ctx(down_share))
    grad_down = down_stack.reshape(ranks * piece, model).astype(f32)
    wide_stack = by_rank(gather_ctx(wide_share))
    spread = functools.partial(spread_kernel, shards_of=owners, ranks=ranks, piece=piece)
    grad_gate, grad_up = call_kernel(
        spread,
        (
            jax.ShapeDtypeStruct((model_part, hidden_width), f32),
            jax.ShapeDtypeStruct((model_part, hidden_width), f32),
        ),
        count=1,
    )(wide_stack)
    grad_out = sum(part.astype(f32) for part in gather_ctx(out_share))
    attn_stack = by_rank(gather_ctx(attn_share))

    def join(start, size):
        return jnp.concatenate(
            [attn_stack[r, :model_part, start : start + size] for r in range(ranks)], axis=1
        ).astype(f32)

    gain_sums = jnp.sum(attn_stack[:, model_part : model_part + 4].astype(f32), axis=0)
    return (
        result[None],
        input_grad[None],
        gain_sums[0, :model_part],
        gain_sums[2, :head_part],
        gain_sums[3, :head_part],
        join(0, q_width),
        join(q_width, kv_width),
        join(q_width + kv_width, kv_width),
        grad_out,
        gain_sums[1, :model_part],
        grad_gate,
        grad_up,
        grad_down,
    )


def solution(mesh):
    return jax.shard_map(
        shards,
        mesh=mesh,
        in_specs=(
            P("fsdp", "ctx", None),
            P("fsdp", "ctx"),
            P(),
            P("fsdp"),
            P("fsdp"),
            P("fsdp"),
            P("fsdp", None),
            P("fsdp", None),
            P("fsdp", None),
            P("fsdp", None),
            P("fsdp"),
            P("fsdp", None),
            P("fsdp", None),
            P("fsdp", None),
            P("fsdp", "ctx", None),
        ),
        out_specs=(
            P("fsdp", "ctx", None),
            P("fsdp", "ctx", None),
            P("fsdp"),
            P("fsdp"),
            P("fsdp"),
            P("fsdp", None),
            P("fsdp", None),
            P("fsdp", None),
            P("fsdp", None),
            P("fsdp"),
            P("fsdp", None),
            P("fsdp", None),
            P("fsdp", None),
        ),
        check_vma=False,
    )
```

time: 1130 us -> 397 us (0.35)
  waiting for transfers between devices: 848 us -> 126 us
  starting transfers between devices: 0.76 us -> 73.6 us
  matrix products: 137 us -> 64.6 us
  blocking collectives: 64 us -> 0 us
  Pallas kernels: 0 us -> 46.2 us
  local copies, waits for them, and re-layouts: 13.3 us -> 35.1 us
  other arithmetic: 45.4 us -> 24.2 us
    reduce_scatter x9 -> x3, waiting for transfers between devices: 440 us -> 0.02 us  [the longest x1 0.02 us: shards(): lax.psum_scatter(out_local, 'fsdp', scatter_dimension=0, tiled=True)]
    all_gather x9 -> x3, waiting for transfers between devices: 334 us -> 0.04 us  [the longest x1 0.02 us: shards(): out_full = lax.all_gather(out_weight, 'fsdp', axis=0, tiled=True)]
    ppermute x0 -> x47, waiting for transfers between devices: none -> 126 us  [the longest x39 98 us: send(): return lax.ppermute(value, 'ctx', [(i, i ^ step) for i in range(ranks)])]
    ppermute x0 -> x47, starting transfers between devices: none -> 73.1 us  [the longest x39 49.6 us: send(): return lax.ppermute(value, 'ctx', [(i, i ^ step) for i in range(ranks)])]
    psum x1 -> x0, waiting for transfers between devices: 69.2 us -> none  [shards(): lax.psum(attn_shares[4].astype(jnp.bfloat16), 'ctx').astype(jnp.float32)]
    pallas_call x0 -> x4, Pallas kernels: none -> 46.2 us  [the longest x1 24.1 us: shards(): call_kernel(functools.partial(attention_backward_kernel, **sizes), (jax.S...]
    dot_general x6 -> x0, matrix products: 45.8 us -> none  [the longest x1 11 us: shards(): jnp.einsum('qgrd,kgd->grqk', mixed_grad, values_all, preferred_element_ty...]
    unnamed x2 -> x0, blocking collectives: 29.8 us -> none
  transfers between devices with their start and end apart: 19 -> 53, of which waited for: 17 -> 22; matrix products, arithmetic and copies ran while one was open for 12% -> 30% of each run, Pallas kernels for 0% -> 11%
where the time goes in v1:
time: 397 us; the launch traced here: 391 us
  waiting for transfers between devices  126 us (32%)
  starting transfers between devices  73.6 us (19%)
  matrix products  64.6 us (16%)
  Pallas kernels  46.2 us (12%)
  local copies, waits for them, and re-layouts  35.1 us (9%)
  other arithmetic  24.2 us (6%)
  between operations  20.8 us (5%)
    ppermute x39, waiting for transfers between devices, send(): return lax.ppermute(value, 'ctx', [(i, i ^ step) for i in range(ranks)])  98 us
    ppermute x39, starting transfers between devices, send(): return lax.ppermute(value, 'ctx', [(i, i ^ step) for i in range(ranks)])  49.6 us
    dot_general x11, matrix products, times_transposed(): lax.dot_general(left, right, (((1,), (1,)), ((), ())), preferred_element_...  28.2 us
    ppermute x8, waiting for transfers between devices, send_owner(): return lax.ppermute(value, 'fsdp', [(i, i ^ step) for i in range(owners)])  27.6 us
    pallas_call x1, Pallas kernels, shards(): call_kernel(functools.partial(attention_backward_kernel, **sizes), (jax.S...  24.1 us
    ppermute x8, starting transfers between devices, send_owner(): return lax.ppermute(value, 'fsdp', [(i, i ^ step) for i in range(owners)])  23.5 us
    dot_general x5, matrix products, dot_plain(): return jnp.dot(left, right, preferred_element_type=jnp.float32)  22.1 us
    pallas_call x1, Pallas kernels, shards(): call_kernel(functools.partial(attention_forward_kernel, **sizes), (jax.Sh...  15 us
  transfers between devices with their start and end apart: 53, of which 22 were waited for; matrix products, arithmetic and copies ran while one was open for 30% of the time, Pallas kernels for 11%

profile of v1, /device:TPU:0, one launch (start us, length us, event | category | flops | bytes accessed | tf_op | source)
XLA Modules:
  0.0 391.0 jit_solution(5005450134765159728)
XLA Ops:
  8.0 2.8 shard_map.247
  10.9 3.0 collective-permute-start
  17.4 2.1 collective-permute-start.6
  30.4 7.0 %collective-permute-done.10 = s32[256]{0:T(256)S(1)} collective-permute-done((s32[256]{0:T(256)S(1)}, s32[256]{0:T(256)S(1)}, u32[]{:S(2)}, u32[]{:S(2)}) %collective-permute-start.10) | collective-permute-done | bytes 1056 | tf_op jit(solution)/shard_map/ppermute | solution.py:265
  40.9 2.6 collective-permute-start.12
  45.4 2.8 collective-permute-start.7
  48.6 3.1 multiply_sine_fusion
  54.8 6.7 %collective-permute-done.8 = bf16[144,512]{1,0:T(8,128)(2,1)S(1)} collective-permute-done((bf16[144,512]{1,0:T(8,128)(2,1)S(1)}, bf16[144,512]{1,0:T(8,128)(2,1)S(1)}, u32[]{:S(2)}, u32[]{:S(2)}) %collective-permute-start.8) | collective-permute-done | bytes 147488 | tf_op jit(solution)/shard_map/ppermute | solution.py:282
  74.3 3.9 %fusion.35.qkv_ref = f32[1024,512]{1,0:T(8,128)} fusion(bf16[1024,512]{1,0:T(8,128)(2,1)} %bitcast.188, bf16[1024,1024]{1,0:T(8,128)(2,1)S(1)} %slice_dynamic-update-slice_fusion, f32[1024]{0:T(1024)S(1)} %bitcast.193, f32[1024]{0:T(1024)S(1)} %add_rsqrt_fusion), kind=kOutput, calls=%fused_computation.71 | convolution fusion | flops 1077936128 | bytes 5251072 | tf_op jit(solution)/shard_map/dot_general | solution.py:23
  78.2 15.0 %shard_map.246 = (bf16[1024,256]{1,0:T(8,128)(2,1)}, bf16[4,1024,64]{2,1,0:T(8,128)(2,1)}, bf16[2,1024,64]{2,1,0:T(8,128)(2,1)}, bf16[2,1024,64]{2,1,0:T(8,128)(2,1)}) custom-call(f32[1024,512]{1,0:T(8,128)} %fusion.35.qkv_ref, f32[1024,128]{1,0:T(8,128)} %get-tuple-element.132.cos_ref, f32[1024,128]{1,0:T(8,128)} %get-tuple-element.131.sin_ref, ...), custom_call_target="tpu_custom_call" | custom-call | tf_op jit(solution)/shard_map/pallas_call | solution.py:395
  94.4 2.4 collective-permute-start.15
  97.6 5.7 %collective-permute-done.13 = bf16[256,256]{1,0:T(8,128)(2,1)S(1)} collective-permute-done((bf16[256,256]{1,0:T(8,128)(2,1)S(1)}, bf16[256,256]{1,0:T(8,128)(2,1)S(1)}, u32[]{:S(2)}, u32[]{:S(2)}) %collective-permute-start.13) | collective-permute-done | bytes 131104 | tf_op jit(solution)/shard_map/ppermute | solution.py:265
  103.8 4.5 %collective-permute-done.14 = bf16[256,256]{1,0:T(8,128)(2,1)S(1)} collective-permute-done((bf16[256,256]{1,0:T(8,128)(2,1)S(1)}, bf16[256,256]{1,0:T(8,128)(2,1)S(1)}, u32[]{:S(2)}, u32[]{:S(2)}) %collective-permute-start.14) | collective-permute-done | bytes 131104 | tf_op jit(solution)/shard_map/ppermute | solution.py:265
  108.4 2.7 multiply_reduce_fusion.2
  119.2 6.9 %collective-permute-done.16 = bf16[256,1024]{1,0:T(8,128)(2,1)S(1)} collective-permute-done((bf16[256,1024]{1,0:T(8,128)(2,1)S(1)}, bf16[256,1024]{1,0:T(8,128)(2,1)S(1)}, u32[]{:S(2)}, u32[]{:S(2)}) %collective-permute-start.16) | collective-permute-done | bytes 524320 | tf_op jit(solution)/shard_map/ppermute | solution.py:265
  126.1 8.9 %collective-permute-done.17 = bf16[256,1024]{1,0:T(8,128)(2,1)S(1)} collective-permute-done((bf16[256,1024]{1,0:T(8,128)(2,1)S(1)}, bf16[256,1024]{1,0:T(8,128)(2,1)S(1)}, u32[]{:S(2)}, u32[]{:S(2)}) %collective-permute-start.17) | collective-permute-done | bytes 524320 | tf_op jit(solution)/shard_map/ppermute | solution.py:265
  135.1 4.9 %fusion.25 = f32[1024,1152]{1,0:T(8,128)S(1)} fusion(bf16[1024,2304]{1,0:T(8,128)(2,1)} %all-gather.8.cloned.1.call-done, bf16[256,1024]{1,0:T(8,128)(2,1)S(1)} %collective-permute-done.18, bf16[256,1024]{1,0:T(8,128)(2,1)S(1)} %collective-permute-done.17, bf16[256,1024]{1,0:T(8,128)(2,1)S(1)} %collective-permute-done.16, ...), kind=kOutput, calls=%fused_computation.47 | convolution fusion | flops 2424307712 | bytes 9175040 | tf_op jit(solution)/shard_map/dot_general | solution.py:23
  140.0 6.5 %multiply_convert_fusion.2 = (bf16[1024,1152]{1,0:T(8,128)(2,1)S(1)}, f32[1024,1152]{1,0:T(8,128)}) fusion(f32[1024,1152]{1,0:T(8,128)S(1)} %fusion.25, bf16[1024,2304]{1,0:T(8,128)(2,1)S(1)} %copy-done.27, bf16[256,1024]{1,0:T(8,128)(2,1)S(1)} %collective-permute-done.18, bf16[256,1024]{1,0:T(8,128)(2,1)S(1)} %collective-permute-done.17, ...), kind=kOutput, calls=%fused_computation.7 | convolution fusion | flops 2431385600 | bytes 16252928 | tf_op jit(solution)/shard_map/dot_general | solution.py:23
  147.9 3.9 convolution_convert_fusion.2
  152.1 9.0 %multiply_convert_fusion = (bf16[1024,1152]{1,0:T(8,128)(2,1)S(1)}, bf16[1024,1152]{1,0:T(8,128)(2,1)S(1)}) fusion(f32[1024,1152]{1,0:T(8,128)} %copy-done.35, f32[1024,1152]{1,0:T(8,128)} %get-tuple-element.140, bf16[1024,1024]{1,0:T(8,128)(2,1)} %copy-done.12, bf16[1152,1024]{1,0:T(8,128)(2,1)} %all-gather.4.cloned.1.call-done), kind=kOutput, calls=%fused_computation.5 | convolution fusion | flops 2431254528 | bytes 18612224 | tf_op jit(solution)/shard_map/dot_general | solution.py:27
  161.1 2.7 fusion.19
  163.8 3.4 fusion.8
  168.2 2.7 fusion.21
  178.4 3.7 convolution_convert_fusion.1
  182.2 3.2 convolution_convert_fusion
  185.4 4.1 %convolution_convert_fusion.3 = bf16[1024,1024]{1,0:T(8,128)(2,1)} fusion(bf16[1024,1152]{1,0:T(8,128)(2,1)S(1)} %copy-done.37, bf16[1152,1024]{1,0:T(8,128)(2,1)S(1)} %copy-done.28), kind=kOutput, calls=%fused_computation.17 | convolution fusion | flops 2416967680 | bytes 6815744 | tf_op jit(solution)/shard_map/dot_general | solution.py:23
  190.3 2.5 pad_maximum_fusion
  192.8 2.1 multiply_reduce_fusion
  201.8 2.1 convolution_convert_fusion.4
  203.8 2.0 collective-permute-done.27
  207.7 2.7 fusion.68
  217.4 24.1 %shard_map.248 = (bf16[1024,512]{1,0:T(8,128)(2,1)}, f32[8,128]{1,0:T(8,128)}) custom-call(f32[1024,512]{1,0:T(8,128)} %fusion.35.qkv_ref, f32[1024,128]{1,0:T(8,128)} %get-tuple-element.132.cos_ref, f32[1024,128]{1,0:T(8,128)} %get-tuple-element.131.sin_ref, f32[1,128]{1,0:T(1,128)} %tile.12.gq_ref, f32[1,128]{1,0:T(1,128)} %tile.28.gk_ref, ...), custom_call_target="tpu_custom_call" | custom-call | tf_op jit(solution)/shard_map/pallas_call | solution.py:466
  242.6 3.7 fusion.4
  252.1 2.4 fusion.48
  254.5 8.7 %collective-permute-done.28 = bf16[256,1024]{1,0:T(8,128)(2,1)S(1)} collective-permute-done((bf16[256,1024]{1,0:T(8,128)(2,1)S(1)}, bf16[256,1024]{1,0:T(8,128)(2,1)S(1)}, u32[]{:S(2)}, u32[]{:S(2)}) %collective-permute-start.28) | collective-permute-done | bytes 524320 | tf_op jit(solution)/shard_map/ppermute | solution.py:265
  263.2 11.5 %collective-permute-done.29 = bf16[256,1024]{1,0:T(8,128)(2,1)S(1)} collective-permute-done((bf16[256,1024]{1,0:T(8,128)(2,1)S(1)}, bf16[256,1024]{1,0:T(8,128)(2,1)S(1)}, u32[]{:S(2)}, u32[]{:S(2)}) %collective-permute-start.29) | collective-permute-done | bytes 524320 | tf_op jit(solution)/shard_map/ppermute | solution.py:265
  276.6 13.7 %collective-permute-start.32 = (bf16[144,512]{1,0:T(8,128)(2,1)S(1)}, bf16[144,512]{1,0:T(8,128)(2,1)S(1)}, u32[]{:S(2)}, u32[]{:S(2)}) collective-permute-start(bf16[144,512]{1,0:T(8,128)(2,1)S(1)} %get-tuple-element.108), channel_id=1, source_target_pairs={{0,2},{1,3},{2,0},{3,1},{4,6},{5,7},{6,4},{7,5},{8,10},{9,11},{10,... | collective-permute-start | bytes 442376 | tf_op jit(solution)/shard_map/ppermute | solution.py:282
  290.3 2.0 collective-permute-start.33
  293.7 9.0 %collective-permute-done.32 = bf16[144,512]{1,0:T(8,128)(2,1)S(1)} collective-permute-done((bf16[144,512]{1,0:T(8,128)(2,1)S(1)}, bf16[144,512]{1,0:T(8,128)(2,1)S(1)}, u32[]{:S(2)}, u32[]{:S(2)}) %collective-permute-start.32) | collective-permute-done | bytes 147488 | tf_op jit(solution)/shard_map/ppermute | solution.py:282
  304.1 9.7 %collective-permute-done.34 = bf16[144,512]{1,0:T(8,128)(2,1)S(1)} collective-permute-done((bf16[144,512]{1,0:T(8,128)(2,1)S(1)}, bf16[144,512]{1,0:T(8,128)(2,1)S(1)}, u32[]{:S(2)}, u32[]{:S(2)}) %collective-permute-start.34) | collective-permute-done | bytes 147488 | tf_op jit(solution)/shard_map/ppermute | solution.py:282
  314.9 2.4 fusion.49
  319.9 5.0 %collective-permute-done.36 = bf16[144,512]{1,0:T(8,128)(2,1)S(1)} collective-permute-done((bf16[144,512]{1,0:T(8,128)(2,1)S(1)}, bf16[144,512]{1,0:T(8,128)(2,1)S(1)}, u32[]{:S(2)}, u32[]{:S(2)}) %collective-permute-start.36) | collective-permute-done | bytes 147488 | tf_op jit(solution)/shard_map/ppermute | solution.py:265
  335.3 2.4 collective-permute-done.44
  339.5 7.3 %collective-permute-done.45 = bf16[144,1024]{1,0:T(8,128)(2,1)S(1)} collective-permute-done((bf16[144,1024]{1,0:T(8,128)(2,1)}, bf16[144,1024]{1,0:T(8,128)(2,1)S(1)}, u32[]{:S(2)}, u32[]{:S(2)}) %collective-permute-start.45) | collective-permute-done | bytes 294944 | tf_op jit(solution)/shard_map/ppermute | solution.py:265
  348.7 4.5 %collective-permute-done.39 = bf16[128,1024]{1,0:T(8,128)(2,1)S(1)} collective-permute-done((bf16[128,1024]{1,0:T(8,128)(2,1)}, bf16[128,1024]{1,0:T(8,128)(2,1)S(1)}, u32[]{:S(2)}, u32[]{:S(2)}) %collective-permute-start.39) | collective-permute-done | bytes 262176 | tf_op jit(solution)/shard_map/ppermute | solution.py:265
  357.9 12.6 %collective-permute-done.41 = bf16[128,2304]{1,0:T(8,128)(2,1)S(1)} collective-permute-done((bf16[128,2304]{1,0:T(8,128)(2,1)}, bf16[128,2304]{1,0:T(8,128)(2,1)S(1)}, u32[]{:S(2)}, u32[]{:S(2)}) %collective-permute-start.41) | collective-permute-done | bytes 589856 | tf_op jit(solution)/shard_map/ppermute | solution.py:265
  370.6 7.5 %collective-permute-done.42 = bf16[128,2304]{1,0:T(8,128)(2,1)S(1)} collective-permute-done((bf16[128,2304]{1,0:T(8,128)(2,1)}, bf16[128,2304]{1,0:T(8,128)(2,1)S(1)}, u32[]{:S(2)}, u32[]{:S(2)}) %collective-permute-start.42) | collective-permute-done | bytes 589856 | tf_op jit(solution)/shard_map/ppermute | solution.py:265
  379.6 4.4 %shard_map.249 = (f32[128,4608]{1,0:T(8,128)}, f32[128,4608]{1,0:T(8,128)}) custom-call(bf16[4,128,2304]{2,1,0:T(8,128)(2,1)} %copy-done.2), custom_call_target="tpu_custom_call" | custom-call | tf_op jit(solution)/shard_map/pallas_call | solution.py:524
  (305 shorter events, 103.9 us)
Async XLA Ops:
  7.2 101.1 %all-gather.6.cloned.1.call-start = ((), (), s32[]{:S(2)}) async-start(), calls=%async_computation.4 | async-start | bytes 2359296 | tf_op jit(solution)/shard_map/all_gather | solution.py:360
  8.0 127.1 %all-gather.8.cloned.1.call-start = ((), (), s32[]{:S(2)}) async-start(), calls=%async_computation.5 | async-start | bytes 5308416 | tf_op jit(solution)/shard_map/all_gather | solution.py:368
  10.8 140.9 %all-gather.4.cloned.1.call-start = ((), (), s32[]{:S(2)}) async-start(), calls=%async_computation.3 | async-start | bytes 2654208 | tf_op jit(solution)/shard_map/all_gather | solution.py:369
  10.9 50.7 %collective-permute-start = (bf16[256,1024]{1,0:T(8,128)(2,1)}, bf16[256,1024]{1,0:T(8,128)(2,1)}, u32[]{:S(2)}, u32[]{:S(2)}) collective-permute-start(bf16[256,1024]{1,0:T(8,128)(2,1)} %bitcast.4), channel_id=1, source_target_pairs={{0,8},{8,0},{16,24},{24,16},{1,9},{9,1},{17,25},{25,17},{2,10},{10... | collective-permute-start | bytes 1572872 | tf_op jit(solution)/shard_map/ppermute | solution.py:265
  13.9 49.7 %collective-permute-start.1 = (bf16[256,1024]{1,0:T(8,128)(2,1)}, bf16[256,1024]{1,0:T(8,128)(2,1)}, u32[]{:S(2)}, u32[]{:S(2)}) collective-permute-start(bf16[256,1024]{1,0:T(8,128)(2,1)} %bitcast.4), channel_id=1, source_target_pairs={{0,16},{8,24},{16,0},{24,8},{1,17},{9,25},{17,1},{25,9},{2,18},{10... | collective-permute-start | bytes 1572872 | tf_op jit(solution)/shard_map/ppermute | solution.py:265
  15.4 50.1 %collective-permute-start.2 = (bf16[256,1024]{1,0:T(8,128)(2,1)}, bf16[256,1024]{1,0:T(8,128)(2,1)}, u32[]{:S(2)}, u32[]{:S(2)}) collective-permute-start(bf16[256,1024]{1,0:T(8,128)(2,1)} %bitcast.4), channel_id=1, source_target_pairs={{0,24},{8,16},{16,8},{24,0},{1,25},{9,17},{17,9},{25,1},{2,26},{10... | collective-permute-start | bytes 1572872 | tf_op jit(solution)/shard_map/ppermute | solution.py:265
  17.4 34.2 %collective-permute-start.6 = (bf16[144,512]{1,0:T(8,128)(2,1)S(1)}, bf16[144,512]{1,0:T(8,128)(2,1)}, u32[]{:S(2)}, u32[]{:S(2)}) collective-permute-start(bf16[144,512]{1,0:T(8,128)(2,1)S(1)} %concatenate.61), channel_id=1, source_target_pairs={{0,2},{1,3},{2,0},{3,1},{4,6},{5,7},{6,4},{7,5},{8,10},{9,11},{10,... | collective-permute-start | bytes 442376 | tf_op jit(solution)/shard_map/ppermute | solution.py:282
  19.5 17.8 %collective-permute-start.10 = (s32[256]{0:T(256)S(1)}, s32[256]{0:T(256)S(1)}, u32[]{:S(2)}, u32[]{:S(2)}) collective-permute-start(s32[256]{0:T(256)S(1)} %bitcast.201), channel_id=1, source_target_pairs={{0,8},{8,0},{16,24},{24,16},{1,9},{9,1},{17,25},{25,17},{2,10},{10... | collective-permute-start | bytes 3080 | tf_op jit(solution)/shard_map/ppermute | solution.py:265
  21.8 305.9 %reduce-scatter.8.cloned.1.call-start = ((), (), s32[]{:S(2)}) async-start(), calls=%async_computation.8 | async-start | bytes 2654208 | tf_op jit(solution)/shard_map/reduce_scatter | solution.py:423
  45.4 9.4 %collective-permute-start.7 = (bf16[144,512]{1,0:T(8,128)(2,1)S(1)}, bf16[144,512]{1,0:T(8,128)(2,1)S(1)}, u32[]{:S(2)}, u32[]{:S(2)}) collective-permute-start(bf16[144,512]{1,0:T(8,128)(2,1)S(1)} %concatenate.61), channel_id=1, source_target_pairs={{0,4},{1,5},{2,6},{3,7},{4,0},{5,1},{6,2},{7,3},{8,12},{9,13},{10,... | collective-permute-start | bytes 442376 | tf_op jit(solution)/shard_map/ppermute | solution.py:282
  51.6 9.9 %collective-permute-start.8 = (bf16[144,512]{1,0:T(8,128)(2,1)S(1)}, bf16[144,512]{1,0:T(8,128)(2,1)S(1)}, u32[]{:S(2)}, u32[]{:S(2)}) collective-permute-start(bf16[144,512]{1,0:T(8,128)(2,1)S(1)} %concatenate.61), channel_id=1, source_target_pairs={{0,6},{1,7},{2,4},{3,5},{4,2},{5,3},{6,0},{7,1},{8,14},{9,15},{10,... | collective-permute-start | bytes 442376 | tf_op jit(solution)/shard_map/ppermute | solution.py:282
  61.5 10.1 %collective-permute-start.9 = (bf16[4,144,512]{2,1,0:T(8,128)(2,1)S(1)}, bf16[4,144,512]{2,1,0:T(8,128)(2,1)S(1)}, u32[]{:S(2)}, u32[]{:S(2)}) collective-permute-start(bf16[4,144,512]{2,1,0:T(8,128)(2,1)S(1)} %bitcast_dynamic-update-slice_fusion.14), channel_id=1, source_target_pairs={{0,1},{1,0},{2,3},{3,2},{4,5},{5,4},{6,7},{7,6},{8,9},{9,8},{10,11... | collective-permute-start | bytes 1769480 | tf_op jit(solution)/shard_map/ppermute | solution.py:282
  67.5 45.7 %collective-permute-start.3 = (bf16[256,1024]{1,0:T(8,128)(2,1)}, bf16[256,1024]{1,0:T(8,128)(2,1)}, u32[]{:S(2)}, u32[]{:S(2)}) collective-permute-start(bf16[256,1024]{1,0:T(8,128)(2,1)} %bitcast.11), channel_id=1, source_target_pairs={{0,8},{8,0},{16,24},{24,16},{1,9},{9,1},{17,25},{25,17},{2,10},{10... | collective-permute-start | bytes 1572872 | tf_op jit(solution)/shard_map/ppermute | solution.py:265
  69.1 47.9 %collective-permute-start.4 = (bf16[256,1024]{1,0:T(8,128)(2,1)}, bf16[256,1024]{1,0:T(8,128)(2,1)}, u32[]{:S(2)}, u32[]{:S(2)}) collective-permute-start(bf16[256,1024]{1,0:T(8,128)(2,1)} %bitcast.11), channel_id=1, source_target_pairs={{0,16},{8,24},{16,0},{24,8},{1,17},{9,25},{17,1},{25,9},{2,18},{10... | collective-permute-start | bytes 1572872 | tf_op jit(solution)/shard_map/ppermute | solution.py:265
  70.5 47.6 %collective-permute-start.5 = (bf16[256,1024]{1,0:T(8,128)(2,1)}, bf16[256,1024]{1,0:T(8,128)(2,1)}, u32[]{:S(2)}, u32[]{:S(2)}) collective-permute-start(bf16[256,1024]{1,0:T(8,128)(2,1)} %bitcast.11), channel_id=1, source_target_pairs={{0,24},{8,16},{16,8},{24,0},{1,25},{9,17},{17,9},{25,1},{2,26},{10... | collective-permute-start | bytes 1572872 | tf_op jit(solution)/shard_map/ppermute | solution.py:265
  94.4 13.8 %collective-permute-start.15 = (bf16[256,256]{1,0:T(8,128)(2,1)S(1)}, bf16[256,256]{1,0:T(8,128)(2,1)S(1)}, u32[]{:S(2)}, u32[]{:S(2)}) collective-permute-start(bf16[256,256]{1,0:T(8,128)(2,1)S(1)} %pad_maximum_fusion.11), channel_id=1, source_target_pairs={{0,24},{8,16},{16,8},{24,0},{1,25},{9,17},{17,9},{25,1},{2,26},{10... | collective-permute-start | bytes 393224 | tf_op jit(solution)/shard_map/ppermute | solution.py:265
  96.8 6.5 %collective-permute-start.13 = (bf16[256,256]{1,0:T(8,128)(2,1)S(1)}, bf16[256,256]{1,0:T(8,128)(2,1)S(1)}, u32[]{:S(2)}, u32[]{:S(2)}) collective-permute-start(bf16[256,256]{1,0:T(8,128)(2,1)S(1)} %pad_maximum_fusion.9), channel_id=1, source_target_pairs={{0,8},{8,0},{16,24},{24,16},{1,9},{9,1},{17,25},{25,17},{2,10},{10... | collective-permute-start | bytes 393224 | tf_op jit(solution)/shard_map/ppermute | solution.py:265
  111.3 14.9 %collective-permute-start.16 = (bf16[256,1024]{1,0:T(8,128)(2,1)S(1)}, bf16[256,1024]{1,0:T(8,128)(2,1)S(1)}, u32[]{:S(2)}, u32[]{:S(2)}) collective-permute-start(bf16[256,1024]{1,0:T(8,128)(2,1)S(1)} %multiply_convert_fusion.3), channel_id=1, source_target_pairs={{0,8},{8,0},{16,24},{24,16},{1,9},{9,1},{17,25},{25,17},{2,10},{10... | collective-permute-start | bytes 1572872 | tf_op jit(solution)/shard_map/ppermute | solution.py:265
  112.6 22.4 %collective-permute-start.17 = (bf16[256,1024]{1,0:T(8,128)(2,1)S(1)}, bf16[256,1024]{1,0:T(8,128)(2,1)S(1)}, u32[]{:S(2)}, u32[]{:S(2)}) collective-permute-start(bf16[256,1024]{1,0:T(8,128)(2,1)S(1)} %multiply_convert_fusion.3), channel_id=1, source_target_pairs={{0,16},{8,24},{16,0},{24,8},{1,17},{9,25},{17,1},{25,9},{2,18},{10... | collective-permute-start | bytes 1572872 | tf_op jit(solution)/shard_map/ppermute | solution.py:265
  113.2 21.8 %collective-permute-start.18 = (bf16[256,1024]{1,0:T(8,128)(2,1)S(1)}, bf16[256,1024]{1,0:T(8,128)(2,1)S(1)}, u32[]{:S(2)}, u32[]{:S(2)}) collective-permute-start(bf16[256,1024]{1,0:T(8,128)(2,1)S(1)} %multiply_convert_fusion.3), channel_id=1, source_target_pairs={{0,24},{8,16},{16,8},{24,0},{1,25},{9,17},{17,9},{25,1},{2,26},{10... | collective-permute-start | bytes 1572872 | tf_op jit(solution)/shard_map/ppermute | solution.py:265
  151.8 181.2 %reduce-scatter.4.cloned.1.call-start = ((), (), s32[]{:S(2)}) async-start(), calls=%async_computation.6 | async-start | bytes 2359296 | tf_op jit(solution)/shard_map/reduce_scatter | solution.py:464
  167.2 25.6 %collective-permute-start.21 = (bf16[256,1024]{1,0:T(8,128)(2,1)}, bf16[256,1024]{1,0:T(8,128)(2,1)S(1)}, u32[]{:S(2)}, u32[]{:S(2)}) collective-permute-start(bf16[256,1024]{1,0:T(8,128)(2,1)} %fusion.8), channel_id=1, source_target_pairs={{0,24},{8,16},{16,8},{24,0},{1,25},{9,17},{17,9},{25,1},{2,26},{10... | collective-permute-start | bytes 1572872 | tf_op jit(solution)/shard_map/ppermute | solution.py:265
  172.6 20.2 %collective-permute-start.20 = (bf16[256,1024]{1,0:T(8,128)(2,1)}, bf16[256,1024]{1,0:T(8,128)(2,1)S(1)}, u32[]{:S(2)}, u32[]{:S(2)}) collective-permute-start(bf16[256,1024]{1,0:T(8,128)(2,1)} %fusion.7), channel_id=1, source_target_pairs={{0,16},{8,24},{16,0},{24,8},{1,17},{9,25},{17,1},{25,9},{2,18},{10... | collective-permute-start | bytes 1572872 | tf_op jit(solution)/shard_map/ppermute | solution.py:265
  176.1 16.8 %collective-permute-start.19 = (bf16[256,1024]{1,0:T(8,128)(2,1)}, bf16[256,1024]{1,0:T(8,128)(2,1)}, u32[]{:S(2)}, u32[]{:S(2)}) collective-permute-start(bf16[256,1024]{1,0:T(8,128)(2,1)} %fusion.6), channel_id=1, source_target_pairs={{0,8},{8,0},{16,24},{24,16},{1,9},{9,1},{17,25},{25,17},{2,10},{10... | collective-permute-start | bytes 1572872 | tf_op jit(solution)/shard_map/ppermute | solution.py:265
  200.0 5.9 %collective-permute-start.27 = (bf16[256,256]{1,0:T(8,128)(2,1)S(1)}, bf16[256,256]{1,0:T(8,128)(2,1)S(1)}, u32[]{:S(2)}, u32[]{:S(2)}) collective-permute-start(bf16[256,256]{1,0:T(8,128)(2,1)S(1)} %get-tuple-element.111), channel_id=1, source_target_pairs={{0,24},{8,16},{16,8},{24,0},{1,25},{9,17},{17,9},{25,1},{2,26},{10... | collective-permute-start | bytes 393224 | tf_op jit(solution)/shard_map/ppermute | solution.py:265
  205.9 148.3 %reduce-scatter.6.cloned.1.call-start = ((), (), s32[]{:S(2)}) async-start(), calls=%async_computation.7 | async-start | bytes 5308416 | tf_op jit(solution)/shard_map/reduce_scatter | solution.py:447
  210.4 39.0 %collective-permute-start.22 = (bf16[256,1024]{1,0:T(8,128)(2,1)}, bf16[256,1024]{1,0:T(8,128)(2,1)S(1)}, u32[]{:S(2)}, u32[]{:S(2)}) collective-permute-start(bf16[256,1024]{1,0:T(8,128)(2,1)} %get-tuple-element.91), channel_id=1, source_target_pairs={{0,8},{8,0},{16,24},{24,16},{1,9},{9,1},{17,25},{25,17},{2,10},{10... | collective-permute-start | bytes 1572872 | tf_op jit(solution)/shard_map/ppermute | solution.py:265
  211.3 39.6 %collective-permute-start.23 = (bf16[256,1024]{1,0:T(8,128)(2,1)}, bf16[256,1024]{1,0:T(8,128)(2,1)}, u32[]{:S(2)}, u32[]{:S(2)}) collective-permute-start(bf16[256,1024]{1,0:T(8,128)(2,1)} %get-tuple-element.90), channel_id=1, source_target_pairs={{0,16},{8,24},{16,0},{24,8},{1,17},{9,25},{17,1},{25,9},{2,18},{10... | collective-permute-start | bytes 1572872 | tf_op jit(solution)/shard_map/ppermute | solution.py:265
  212.8 39.3 %collective-permute-start.24 = (bf16[256,1024]{1,0:T(8,128)(2,1)}, bf16[256,1024]{1,0:T(8,128)(2,1)}, u32[]{:S(2)}, u32[]{:S(2)}) collective-permute-start(bf16[256,1024]{1,0:T(8,128)(2,1)} %get-tuple-element.89), channel_id=1, source_target_pairs={{0,24},{8,16},{16,8},{24,0},{1,25},{9,17},{17,9},{25,1},{2,26},{10... | collective-permute-start | bytes 1572872 | tf_op jit(solution)/shard_map/ppermute | solution.py:265
  248.0 28.3 %collective-permute-start.31 = (bf16[4,144,512]{2,1,0:T(8,128)(2,1)S(1)}, bf16[4,144,512]{2,1,0:T(8,128)(2,1)S(1)}, u32[]{:S(2)}, u32[]{:S(2)}) collective-permute-start(bf16[4,144,512]{2,1,0:T(8,128)(2,1)S(1)} %select_bitcast_fusion), channel_id=1, source_target_pairs={{0,1},{1,0},{2,3},{3,2},{4,5},{5,4},{6,7},{7,6},{8,9},{9,8},{10,11... | collective-permute-start | bytes 1769480 | tf_op jit(solution)/shard_map/ppermute | solution.py:282
  248.4 14.9 %collective-permute-start.28 = (bf16[256,1024]{1,0:T(8,128)(2,1)S(1)}, bf16[256,1024]{1,0:T(8,128)(2,1)S(1)}, u32[]{:S(2)}, u32[]{:S(2)}) collective-permute-start(bf16[256,1024]{1,0:T(8,128)(2,1)S(1)} %pad_maximum_fusion.5), channel_id=1, source_target_pairs={{0,8},{8,0},{16,24},{24,16},{1,9},{9,1},{17,25},{25,17},{2,10},{10... | collective-permute-start | bytes 1572872 | tf_op jit(solution)/shard_map/ppermute | solution.py:265
  249.5 25.3 %collective-permute-start.29 = (bf16[256,1024]{1,0:T(8,128)(2,1)S(1)}, bf16[256,1024]{1,0:T(8,128)(2,1)S(1)}, u32[]{:S(2)}, u32[]{:S(2)}) collective-permute-start(bf16[256,1024]{1,0:T(8,128)(2,1)S(1)} %pad_maximum_fusion.6), channel_id=1, source_target_pairs={{0,16},{8,24},{16,0},{24,8},{1,17},{9,25},{17,1},{25,9},{2,18},{10... | collective-permute-start | bytes 1572872 | tf_op jit(solution)/shard_map/ppermute | solution.py:265
  251.0 23.8 %collective-permute-start.30 = (bf16[256,1024]{1,0:T(8,128)(2,1)S(1)}, bf16[256,1024]{1,0:T(8,128)(2,1)S(1)}, u32[]{:S(2)}, u32[]{:S(2)}) collective-permute-start(bf16[256,1024]{1,0:T(8,128)(2,1)S(1)} %pad_maximum_fusion.7), channel_id=1, source_target_pairs={{0,24},{8,16},{16,8},{24,0},{1,25},{9,17},{17,9},{25,1},{2,26},{10... | collective-permute-start | bytes 1572872 | tf_op jit(solution)/shard_map/ppermute | solution.py:265
  276.6 26.1 %collective-permute-start.32 = (bf16[144,512]{1,0:T(8,128)(2,1)S(1)}, bf16[144,512]{1,0:T(8,128)(2,1)S(1)}, u32[]{:S(2)}, u32[]{:S(2)}) collective-permute-start(bf16[144,512]{1,0:T(8,128)(2,1)S(1)} %get-tuple-element.108), channel_id=1, source_target_pairs={{0,2},{1,3},{2,0},{3,1},{4,6},{5,7},{6,4},{7,5},{8,10},{9,11},{10,... | collective-permute-start | bytes 442376 | tf_op jit(solution)/shard_map/ppermute | solution.py:282
  290.3 13.7 %collective-permute-start.33 = (bf16[144,512]{1,0:T(8,128)(2,1)S(1)}, bf16[144,512]{1,0:T(8,128)(2,1)S(1)}, u32[]{:S(2)}, u32[]{:S(2)}) collective-permute-start(bf16[144,512]{1,0:T(8,128)(2,1)S(1)} %get-tuple-element.110), channel_id=1, source_target_pairs={{0,4},{1,5},{2,6},{3,7},{4,0},{5,1},{6,2},{7,3},{8,12},{9,13},{10,... | collective-permute-start | bytes 442376 | tf_op jit(solution)/shard_map/ppermute | solution.py:282
  292.3 21.5 %collective-permute-start.34 = (bf16[144,512]{1,0:T(8,128)(2,1)S(1)}, bf16[144,512]{1,0:T(8,128)(2,1)S(1)}, u32[]{:S(2)}, u32[]{:S(2)}) collective-permute-start(bf16[144,512]{1,0:T(8,128)(2,1)S(1)} %get-tuple-element.109), channel_id=1, source_target_pairs={{0,6},{1,7},{2,4},{3,5},{4,2},{5,3},{6,0},{7,1},{8,14},{9,15},{10,... | collective-permute-start | bytes 442376 | tf_op jit(solution)/shard_map/ppermute | solution.py:282
  313.9 5.9 %collective-permute-start.35 = (bf16[144,512]{1,0:T(8,128)(2,1)S(1)}, bf16[144,512]{1,0:T(8,128)(2,1)S(1)}, u32[]{:S(2)}, u32[]{:S(2)}) collective-permute-start(bf16[144,512]{1,0:T(8,128)(2,1)S(1)} %get-tuple-element.74), channel_id=1, source_target_pairs={{0,8},{8,0},{16,24},{24,16},{1,9},{9,1},{17,25},{25,17},{2,10},{10... | collective-permute-start | bytes 442376 | tf_op jit(solution)/shard_map/ppermute | solution.py:265
  317.3 7.6 %collective-permute-start.36 = (bf16[144,512]{1,0:T(8,128)(2,1)S(1)}, bf16[144,512]{1,0:T(8,128)(2,1)S(1)}, u32[]{:S(2)}, u32[]{:S(2)}) collective-permute-start(bf16[144,512]{1,0:T(8,128)(2,1)S(1)} %get-tuple-element.74), channel_id=1, source_target_pairs={{0,16},{8,24},{16,0},{24,8},{1,17},{9,25},{17,1},{25,9},{2,18},{10... | collective-permute-start | bytes 442376 | tf_op jit(solution)/shard_map/ppermute | solution.py:265
  318.6 6.4 %collective-permute-start.37 = (bf16[144,512]{1,0:T(8,128)(2,1)S(1)}, bf16[144,512]{1,0:T(8,128)(2,1)S(1)}, u32[]{:S(2)}, u32[]{:S(2)}) collective-permute-start(bf16[144,512]{1,0:T(8,128)(2,1)S(1)} %get-tuple-element.74), channel_id=1, source_target_pairs={{0,24},{8,16},{16,8},{24,0},{1,25},{9,17},{17,9},{25,1},{2,26},{10... | collective-permute-start | bytes 442376 | tf_op jit(solution)/shard_map/ppermute | solution.py:265
  327.7 10.1 %collective-permute-start.44 = (bf16[144,1024]{1,0:T(8,128)(2,1)}, bf16[144,1024]{1,0:T(8,128)(2,1)S(1)}, u32[]{:S(2)}, u32[]{:S(2)}) collective-permute-start(bf16[144,1024]{1,0:T(8,128)(2,1)} %reduce-scatter.8.cloned.1.call-done), channel_id=1, source_target_pairs={{0,8},{8,0},{16,24},{24,16},{1,9},{9,1},{17,25},{25,17},{2,10},{10... | collective-permute-start | bytes 884744 | tf_op jit(solution)/shard_map/ppermute | solution.py:265
  329.7 17.1 %collective-permute-start.45 = (bf16[144,1024]{1,0:T(8,128)(2,1)}, bf16[144,1024]{1,0:T(8,128)(2,1)S(1)}, u32[]{:S(2)}, u32[]{:S(2)}) collective-permute-start(bf16[144,1024]{1,0:T(8,128)(2,1)} %reduce-scatter.8.cloned.1.call-done), channel_id=1, source_target_pairs={{0,16},{8,24},{16,0},{24,8},{1,17},{9,25},{17,1},{25,9},{2,18},{10... | collective-permute-start | bytes 884744 | tf_op jit(solution)/shard_map/ppermute | solution.py:265
  330.6 16.1 %collective-permute-start.46 = (bf16[144,1024]{1,0:T(8,128)(2,1)}, bf16[144,1024]{1,0:T(8,128)(2,1)S(1)}, u32[]{:S(2)}, u32[]{:S(2)}) collective-permute-start(bf16[144,1024]{1,0:T(8,128)(2,1)} %reduce-scatter.8.cloned.1.call-done), channel_id=1, source_target_pairs={{0,24},{8,16},{16,8},{24,0},{1,25},{9,17},{17,9},{25,1},{2,26},{10... | collective-permute-start | bytes 884744 | tf_op jit(solution)/shard_map/ppermute | solution.py:265
  333.0 15.7 %collective-permute-start.38 = (bf16[128,1024]{1,0:T(8,128)(2,1)}, bf16[128,1024]{1,0:T(8,128)(2,1)S(1)}, u32[]{:S(2)}, u32[]{:S(2)}) collective-permute-start(bf16[128,1024]{1,0:T(8,128)(2,1)} %reduce-scatter.4.cloned.1.call-done), channel_id=1, source_target_pairs={{0,8},{8,0},{16,24},{24,16},{1,9},{9,1},{17,25},{25,17},{2,10},{10... | collective-permute-start | bytes 786440 | tf_op jit(solution)/shard_map/ppermute | solution.py:265
  334.4 18.9 %collective-permute-start.39 = (bf16[128,1024]{1,0:T(8,128)(2,1)}, bf16[128,1024]{1,0:T(8,128)(2,1)S(1)}, u32[]{:S(2)}, u32[]{:S(2)}) collective-permute-start(bf16[128,1024]{1,0:T(8,128)(2,1)} %reduce-scatter.4.cloned.1.call-done), channel_id=1, source_target_pairs={{0,16},{8,24},{16,0},{24,8},{1,17},{9,25},{17,1},{25,9},{2,18},{10... | collective-permute-start | bytes 786440 | tf_op jit(solution)/shard_map/ppermute | solution.py:265
  337.8 15.5 %collective-permute-start.40 = (bf16[128,1024]{1,0:T(8,128)(2,1)}, bf16[128,1024]{1,0:T(8,128)(2,1)S(1)}, u32[]{:S(2)}, u32[]{:S(2)}) collective-permute-start(bf16[128,1024]{1,0:T(8,128)(2,1)} %reduce-scatter.4.cloned.1.call-done), channel_id=1, source_target_pairs={{0,24},{8,16},{16,8},{24,0},{1,25},{9,17},{17,9},{25,1},{2,26},{10... | collective-permute-start | bytes 786440 | tf_op jit(solution)/shard_map/ppermute | solution.py:265
  354.2 16.3 %collective-permute-start.41 = (bf16[128,2304]{1,0:T(8,128)(2,1)}, bf16[128,2304]{1,0:T(8,128)(2,1)S(1)}, u32[]{:S(2)}, u32[]{:S(2)}) collective-permute-start(bf16[128,2304]{1,0:T(8,128)(2,1)} %reduce-scatter.6.cloned.1.call-done), channel_id=1, source_target_pairs={{0,8},{8,0},{16,24},{24,16},{1,9},{9,1},{17,25},{25,17},{2,10},{10... | collective-permute-start | bytes 1769480 | tf_op jit(solution)/shard_map/ppermute | solution.py:265
  355.8 22.3 %collective-permute-start.42 = (bf16[128,2304]{1,0:T(8,128)(2,1)}, bf16[128,2304]{1,0:T(8,128)(2,1)S(1)}, u32[]{:S(2)}, u32[]{:S(2)}) collective-permute-start(bf16[128,2304]{1,0:T(8,128)(2,1)} %reduce-scatter.6.cloned.1.call-done), channel_id=1, source_target_pairs={{0,16},{8,24},{16,0},{24,8},{1,17},{9,25},{17,1},{25,9},{2,18},{10... | collective-permute-start | bytes 1769480 | tf_op jit(solution)/shard_map/ppermute | solution.py:265
  355.8 22.3 %collective-permute-start.43 = (bf16[128,2304]{1,0:T(8,128)(2,1)}, bf16[128,2304]{1,0:T(8,128)(2,1)S(1)}, u32[]{:S(2)}, u32[]{:S(2)}) collective-permute-start(bf16[128,2304]{1,0:T(8,128)(2,1)} %reduce-scatter.6.cloned.1.call-done), channel_id=1, source_target_pairs={{0,24},{8,16},{16,8},{24,0},{1,25},{9,17},{17,9},{25,1},{2,26},{10... | collective-permute-start | bytes 1769480 | tf_op jit(solution)/shard_map/ppermute | solution.py:265
  (45 other events, 275.2 us)
Sparse Core Ops, SparseCore 0:
  9.7 31.3 all-gather.5
  43.3 55.9 all-gather.7
  100.9 32.0 all-gather.3
  151.9 48.7 reduce-scatter.7
  206.0 48.5 reduce-scatter.3
  256.7 62.9 reduce-scatter.5
